TPU v7x, 32 devices: a whole 2x2x4 slice. The times are simulated.
32 devices in a mesh: clips: 2 (over x), tm: 8 (over z, y), head: 2 (over core).
Axes of the slice: x: 2, y: 2, z: 4, core: 2. Of those that a mesh axis runs over, the one named last changes fastest.
Arguments:
- query: bfloat16 [12288, 3072], P(('clips', 'tm'), 'head'), parts along dimension 0, may hold values from -24 to 24
- key: bfloat16 [12288, 3072], P(('clips', 'tm'), 'head'), parts along dimension 0, may hold values from -12 to 12
- value: bfloat16 [12288, 3072], P(('clips', 'tm'), 'head'), parts along dimension 0, may hold values from -6 to 6
- tile_mask: int32 [16, 6, 27], P(('clips', 'tm')), parts along dimension 0, may hold values from 0 to 1, as said below
- order: int32 [16, 768], P(('clips', 'tm')), parts along dimension 0, may hold values from 0 to 767, each once within a row
- out_weight: bfloat16 [3072, 3072], P(None, 'tm'), may hold values from -0.109375 to 0.109375
Outputs:
- mixed: bfloat16 [12288, 3072], P(('clips', 'tm', 'head')), parts along dimension 0
There are 2 independent parts, one for each index of `clips`. A program takes and returns all parts, laid end to end along the dimension named above; an argument that names none is the same for every part. Nothing has to cross between parts.
Inputs may be any that keep to these rules, and one draw needn't show every extreme that they name: `tile_mask`: the tile itself (slot 13) is always 1; slots of neighbours outside the grid of 8 x 2 x 3 tiles are 0. `order`: each row is a permutation of the 768 rows of one time tile's block.
All inputs are finite; a program needn't handle non-finite values.
Results may differ from a plain program's by a relative error of at most 0.0052.
Values may be sent and summed in bfloat16 or wider, within the bound.
A program may use at most 128 MiB of HBM per device.

v0:
```python
import jax
import jax.numpy as jnp
from jax import lax
from jax.sharding import PartitionSpec as P

HD = 128
GW = 3


def with_halo(block, sides, width):
    for axis, dim in sides:
        count = lax.axis_size(axis)
        forward = [(i, i + 1) for i in range(count - 1)]
        backward = [(target, source) for source, target in forward]
        low = lax.ppermute(
            lax.slice_in_dim(block, block.shape[dim] - width, None, axis=dim), axis, forward
        )
        high = lax.ppermute(lax.slice_in_dim(block, 0, width, axis=dim), axis, backward)
        block = jnp.concatenate([low, block, high], axis=dim)
    return block


def allowed_tiles(mask_rows, first_tile, total_tiles):
    count = mask_rows.shape[0]
    tiles = jnp.arange(count, dtype=jnp.int32)
    row_diff = tiles[None, :] // GW - tiles[:, None] // GW
    col_diff = tiles[None, :] % GW - tiles[:, None] % GW
    near = (jnp.abs(row_diff) <= 1) & (jnp.abs(col_diff) <= 1)
    slots = jnp.arange(27, dtype=jnp.int32)
    blocks = []
    for shift_time in (-1, 0, 1):
        slot = (
            (shift_time + 1) * 9
            + (jnp.clip(row_diff, -1, 1) + 1) * 3
            + jnp.clip(col_diff, -1, 1)
            + 1
        )
        picked = jnp.sum(
            jnp.where(slot[:, :, None] == slots[None, None, :], mask_rows[:, None, :], 0), axis=2
        )
        inside = (first_tile + shift_time >= 0) & (first_tile + shift_time < total_tiles)
        blocks.append(near & (picked == 1) & inside)
    return jnp.stack(blocks, axis=1)


def attend(queries, keys, values, allowed, tile_tok):
    rows = queries.shape[0]
    width = queries.shape[1]
    heads = width // HD
    count = allowed.shape[0]
    head_queries = queries.reshape(rows, heads, HD).transpose(1, 0, 2)
    head_keys = keys.reshape(3 * rows, heads, HD).transpose(1, 0, 2)
    head_values = values.reshape(3 * rows, heads, HD).transpose(1, 0, 2)
    visible = allowed.reshape(count, 1, 3 * count, 1)
    scale = HD ** (-0.5)

    def one_head(inputs):
        part_q, part_k, part_v = inputs
        scores = jnp.dot(part_q, part_k.T, preferred_element_type=jnp.float32) * scale
        scores = scores.reshape(count, tile_tok, 3 * count, tile_tok)
        scores = jnp.where(visible, scores, -jnp.inf)
        top = jnp.max(scores, axis=(2, 3), keepdims=True)
        expon = jnp.exp(scores - top)
        denom = jnp.sum(expon, axis=(2, 3)).reshape(rows, 1)
        weights = expon.reshape(rows, 3 * rows).astype(jnp.bfloat16)
        result = jnp.dot(weights, part_v, preferred_element_type=jnp.float32) / denom
        return result.astype(jnp.bfloat16)

    outputs = lax.map(one_head, (head_queries, head_keys, head_values))
    return outputs.transpose(1, 0, 2).reshape(rows, width)


def on_device(query, key, value, tile_mask, order, out_weight):
    local_tiles = tile_mask.shape[0]
    slab = order.shape[1]
    width = query.shape[1]
    tile_tok = slab // tile_mask.shape[1]

    def to_tiles(data):
        blocks = data.reshape(local_tiles, slab, width)
        return jnp.take_along_axis(blocks, order[:, :, None], axis=1)

    queries = to_tiles(query)
    joined = jnp.stack([to_tiles(key), to_tiles(value)], axis=1)
    padded = with_halo(joined, (("tm", 0),), 1)
    first = lax.axis_index("tm") * local_tiles
    total = local_tiles * lax.axis_size("tm")
    allowed = allowed_tiles(tile_mask[0], first + 0, total)
    window_keys = padded[:, 0].reshape(3 * slab, width)
    window_values = padded[:, 1].reshape(3 * slab, width)
    results = [attend(queries[0], window_keys, window_values, allowed, tile_tok)]
    tiled = jnp.stack(results, axis=0)
    restored = (
        jnp.zeros_like(tiled)
        .at[jnp.arange(local_tiles, dtype=jnp.int32)[:, None], order]
        .set(tiled)
    )
    restored = restored.reshape(local_tiles * slab, width)
    all_heads = lax.all_to_all(restored, "head", split_axis=0, concat_axis=1, tiled=True)
    mixed = jnp.dot(
        all_heads,
        lax.all_gather(out_weight, "tm", axis=1, tiled=True),
        preferred_element_type=jnp.float32,
    )
    return mixed.astype(jnp.bfloat16)


def solution(mesh):
    placed = (
        P(("clips", "tm"), "head"),
        P(("clips", "tm"), "head"),
        P(("clips", "tm"), "head"),
        P(("clips", "tm"), None, None),
        P(("clips", "tm"), None),
        P(None, "tm"),
    )
    return jax.shard_map(
        on_device,
        mesh=mesh,
        in_specs=placed,
        out_specs=P(("clips", "tm", "head"), None),
        check_vma=False,
    )
```

profile of v0, /device:TPU:0, one launch (start us, length us, event | category | flops | bytes accessed | tf_op | source)
XLA Modules:
  0.0 639.2 jit_solution(823696893544403984)
XLA Ops:
  8.2 3.8 gather_fusion
  12.0 8.0 %gather_fusion.1 = bf16[768,1536]{1,0:T(8,128)(2,1)} fusion(bf16[768,1536]{1,0:T(8,128)(2,1)} %param.11, s32[1024]{0:T(1024)S(1)} %pad_clamp_fusion), kind=kCustom, calls=%fused_computation.1.clone | custom fusion | bytes 4721664 | tf_op jit(solution)/shard_map/jit(take_along_axis)/gather | solution.py:81
  20.1 3.9 gather_fusion.2
  23.9 4.6 fusion.23
  28.5 2.9 pad_maximum_fusion.1
  31.4 7.1 %collective-permute-start = (bf16[1,2,768,1536]{3,2,1,0:T(8,128)(2,1)}, bf16[1,2,768,1536]{3,2,1,0:T(8,128)(2,1)}, u32[]{:S(2)}, u32[]{:S(2)}) collective-permute-start(bf16[1,2,768,1536]{3,2,1,0:T(8,128)(2,1)} %pad_maximum_fusion.1), channel_id=1, source_target_pairs={{0,2},{2,4},{4,6},{6,8},{8,10},{10,12},{12,14},{1,3},{3,5},{5,7},{... | collective-permute-start | bytes 14155784 | tf_op jit(solution)/shard_map/ppermute | solution.py:15
  38.5 1.5 collective-permute-start.1
  40.8 4.3 copy.26
  45.1 399.2 %collective-permute-done = bf16[1,2,768,1536]{3,2,1,0:T(8,128)(2,1)} collective-permute-done((bf16[1,2,768,1536]{3,2,1,0:T(8,128)(2,1)}, bf16[1,2,768,1536]{3,2,1,0:T(8,128)(2,1)}, u32[]{:S(2)}, u32[]{:S(2)}) %collective-permute-start) | collective-permute-done | bytes 4718624 | tf_op jit(solution)/shard_map/ppermute | solution.py:15
  444.3 6.9 %pad_maximum_fusion = bf16[3,2,768,1536]{3,2,1,0:T(8,128)(2,1)S(1)} fusion(bf16[1,2,768,1536]{3,2,1,0:T(8,128)(2,1)} %collective-permute-done.1, bf16[1,1,768,1536]{3,2,1,0:T(8,128)(2,1)} %copy-done.3, bf16[1,1,768,1536]{3,2,1,0:T(8,128)(2,1)S(1)} %get-tuple-element.76, bf16[1,2,768,1536]{3,2,1,0:T(8,128)(2,1)} %collective-permute-done), kind=kLoop, calls=%fused_computation.22 | loop fusion | flops 21233664 | bytes 28311552 | tf_op jit(solution)/shard_map/concatenate | solution.py:19
  451.2 5.6 fusion.34
  456.8 13.6 %reshape_reshape_squeeze.6 = bf16[2304,12,128]{2,1,0:T(8,128)(2,1)} reshape(bf16[3,1,768,1536]{3,2,1,0:T(8,128)(2,1)} %get-tuple-element.75) | data formatting | bytes 14155776 | tf_op jit(solution)/shard_map/reshape;reshape;squeeze | solution.py:52
  470.4 8.4 %copy.28 = bf16[12,2304,128]{2,1,0:T(8,128)(2,1)} copy(bf16[12,2304,128]{2,0,1:T(8,128)(2,1)} %bitcast.93) | data formatting | bytes 14155776 | tf_op jit(solution)/shard_map/while | solution.py:69
  478.9 13.6 %reshape_reshape_squeeze.7 = bf16[2304,12,128]{2,1,0:T(8,128)(2,1)} reshape(bf16[3,1,768,1536]{3,2,1,0:T(8,128)(2,1)} %get-tuple-element.74) | data formatting | bytes 14155776 | tf_op jit(solution)/shard_map/reshape;reshape;squeeze | solution.py:53
  492.5 8.4 %copy.29 = bf16[12,2304,128]{2,1,0:T(8,128)(2,1)} copy(bf16[12,2304,128]{2,0,1:T(8,128)(2,1)} %bitcast.94) | data formatting | bytes 14155776 | tf_op jit(solution)/shard_map/while | solution.py:69
  500.9 95.4 %while.10 = (s32[]{:T(128)}, bf16[12,768,128]{1,2,0:T(8,128)(2,1)}, pred[6,1,18,1]{2,0,3,1:T(8,128)(4,1)S(1)}, bf16[12,768,128]{1,2,0:T(8,128)(2,1)}, bf16[12,23...) while((s32[]{:T(128)}, bf16[12,768,128]{1,2,0:T(8,128)(2,1)}, ...), condition=%wide.region_6.8_spmd, body=%wide.region_3.7_spmd.sunk | while | flops 918551040 | bytes 27149496 | solution.py:69
  501.6 3.0 fusion.44
  504.6 1.1 fusion.45
  505.7 2.3 fusion.46
  509.5 3.0 fusion.44
  512.6 1.1 fusion.45
  513.7 2.3 fusion.46
  517.5 3.0 fusion.44
  520.5 1.1 fusion.45
  521.6 2.3 fusion.46
  525.4 3.0 fusion.44
  529.6 2.3 fusion.46
  533.4 3.0 fusion.44
  537.5 2.3 fusion.46
  541.3 3.0 fusion.44
  545.5 2.3 fusion.46
  549.3 3.0 fusion.44
  553.4 2.3 fusion.46
  557.2 3.0 fusion.44
  561.4 2.3 fusion.46
  565.2 3.0 fusion.44
  569.3 2.3 fusion.46
  573.1 3.0 fusion.44
  577.3 2.3 fusion.46
  581.1 3.0 fusion.44
  585.2 2.3 fusion.46
  589.0 3.0 fusion.44
  593.2 2.3 fusion.46
  596.3 4.3 copy.31
  600.6 7.7 %scatter_custom_fusion = bf16[768,1536]{1,0:T(8,128)(2,1)S(1)} fusion(s32[768]{0:T(1024)S(1)} %fusion.30, bf16[768,1536]{1,0:T(8,128)(2,1)} %copy.31, bf16[]{:T(256)} %constant.48.clone.1), kind=kCustom, calls=%fused_computation.30 | custom fusion | bytes 2359808 | tf_op jit(solution)/shard_map/scatter | solution.py:96
  608.3 6.5 %all_to_all.19 = bf16[2,384,1536]{2,1,0:T(8,128)(2,1)} all-to-all(bf16[2,384,1536]{2,1,0:T(8,128)(2,1)S(1)} %bitcast.95), channel_id=1, replica_groups=mesh['clips'=2,'tm'=8,'head'=2] {'head'}, dimensions={0} | all-to-all | bytes 4718592 | tf_op jit(solution)/shard_map/all_to_all | solution.py:99
  614.8 4.3 copy.32
  619.1 13.3 %convolution_convert_fusion = bf16[384,3072]{1,0:T(8,128)(2,1)} fusion(bf16[384,3072]{0,1:T(8,128)(2,1)} %bitcast.99, bf16[3072,3072]{1,0:T(8,128)(2,1)} %all-gather.2.cloned.1.call-done), kind=kOutput, calls=%fused_computation.24 | convolution fusion | flops 7248936960 | bytes 23592960 | tf_op jit(solution)/shard_map/dot_general | solution.py:100
  (76 shorter events, 30.6 us)
Async XLA Ops:
  6.5 1.7 copy-start
  6.5 0.8 copy-start.4
  6.5 612.5 %all-gather.2.cloned.1.call-start = ((), (), s32[]{:S(2)}) async-start(), calls=%async_computation.1 | async-start | bytes 21233664 | tf_op jit(solution)/shard_map/all_gather | solution.py:102
  12.0 8.0 %copy-start.2 = (bf16[768,1536]{1,0:T(8,128)(2,1)S(1)}, bf16[768,1536]{1,0:T(8,128)(2,1)}, u32[]{:S(2)}) copy-start(bf16[768,1536]{1,0:T(8,128)(2,1)} %param.12) | copy-start | bytes 7077892
  28.5 2.9 copy-start.3
  28.5 11.5 %copy-start.5 = (s32[1,6,27]{2,0,1:T(1,128)S(1)}, s32[1,6,27]{2,0,1:T(1,128)}, u32[]{:S(2)}) copy-start(s32[1,6,27]{2,0,1:T(1,128)} %param.13) | copy-start | bytes 1948
  31.4 412.9 %collective-permute-start = (bf16[1,2,768,1536]{3,2,1,0:T(8,128)(2,1)}, bf16[1,2,768,1536]{3,2,1,0:T(8,128)(2,1)}, u32[]{:S(2)}, u32[]{:S(2)}) collective-permute-start(bf16[1,2,768,1536]{3,2,1,0:T(8,128)(2,1)} %pad_maximum_fusion.1), channel_id=1, source_target_pairs={{0,2},{2,4},{4,6},{6,8},{8,10},{10,12},{12,14},{1,3},{3,5},{5,7},{... | collective-permute-start | bytes 14155784 | tf_op jit(solution)/shard_map/ppermute | solution.py:15
  38.5 405.8 %collective-permute-start.1 = (bf16[1,2,768,1536]{3,2,1,0:T(8,128)(2,1)}, bf16[1,2,768,1536]{3,2,1,0:T(8,128)(2,1)}, u32[]{:S(2)}, u32[]{:S(2)}) collective-permute-start(bf16[1,2,768,1536]{3,2,1,0:T(8,128)(2,1)} %pad_maximum_fusion.1), channel_id=1, source_target_pairs={{2,0},{4,2},{6,4},{8,6},{10,8},{12,10},{14,12},{3,1},{5,3},{7,5},{... | collective-permute-start | bytes 14155784 | tf_op jit(solution)/shard_map/ppermute | solution.py:18
  619.1 13.3 %copy-start.1 = (bf16[768,1536]{1,0:T(8,128)(2,1)S(1)}, bf16[768,1536]{1,0:T(8,128)(2,1)}, u32[]{:S(2)}) copy-start(bf16[768,1536]{1,0:T(8,128)(2,1)} %param.10) | copy-start | bytes 7077892
Sparse Core Ops, SparseCore 0:
  8.9 564.7 all-gather.1
where the time goes:
time: 641 us; the launch traced here: 639 us
  waiting for transfers between devices  400 us (62%)
  local copies, waits for them, and re-layouts  105 us (16%)
  matrix products  77 us (12%)
  other arithmetic  28.2 us (4%)
  between operations  13.5 us (2%)
  starting transfers between devices  8.57 us (1%)
  blocking collectives  6.54 us (1%)
    ppermute x1, waiting for transfers between devices, with_halo(): lax.ppermute(lax.slice_in_dim(block, block.shape[dim] - width, None, axis...  399 us
    dot_general x12, matrix products, one_head(): jnp.dot(part_q, part_k.T, preferred_element_type=jnp.float32) * scale  36.5 us
    dot_general x12, matrix products, one_head(): jnp.dot(weights, part_v, preferred_element_type=jnp.float32) / denom  27.2 us
    while x2, local copies, waits for them, and re-layouts, attend(): outputs = lax.map(one_head, (head_queries, head_keys, head_values))  16.8 us
    gather x3, local copies, waits for them, and re-layouts, to_tiles(): return jnp.take_along_axis(blocks, order[:, :, None], axis=1)  15.7 us
    another operation x1, local copies, waits for them, and re-layouts, attend(): head_values = values.reshape(3 * rows, heads, HD).transpose(1, 0, 2)  13.6 us
    another operation x1, local copies, waits for them, and re-layouts, attend(): head_keys = keys.reshape(3 * rows, heads, HD).transpose(1, 0, 2)  13.6 us
    dot_general x1, matrix products, on_device(): jnp.dot(all_heads, lax.all_gather(out_weight, 'tm', axis=1, tiled=True),...  13.3 us
  transfers between devices with their start and end apart: 3, of which 1 were waited for; matrix products, arithmetic and copies ran while one was open for 31% of the time, Pallas kernels for 0%

commit v1 on v0

v1 whole, which is shorter than its diff:
```python
import functools
import math

import jax
import jax.numpy as jnp
from jax import lax
from jax.experimental import pallas as pl
from jax.experimental.pallas import tpu as pltpu
from jax.sharding import PartitionSpec as P

HD = 128
GW = 3
CHUNK_HEADS = 2
HIDDEN = -1e30


def allowed_tiles(mask_rows, first_tile, total_tiles):
    count = mask_rows.shape[0]
    tiles = jnp.arange(count, dtype=jnp.int32)
    row_diff = tiles[None, :] // GW - tiles[:, None] // GW
    col_diff = tiles[None, :] % GW - tiles[:, None] % GW
    near = (jnp.abs(row_diff) <= 1) & (jnp.abs(col_diff) <= 1)
    slots = jnp.arange(27, dtype=jnp.int32)
    blocks = []
    for shift_time in (-1, 0, 1):
        slot = (
            (shift_time + 1) * 9
            + (jnp.clip(row_diff, -1, 1) + 1) * 3
            + jnp.clip(col_diff, -1, 1)
            + 1
        )
        picked = jnp.sum(
            jnp.where(slot[:, :, None] == slots[None, None, :], mask_rows[:, None, :], 0), axis=2
        )
        inside = (first_tile + shift_time >= 0) & (first_tile + shift_time < total_tiles)
        blocks.append(near & (picked == 1) & inside)
    return blocks


def reorder_kernel(pick_ref, a_ref, o_ref):
    o_ref[...] = jnp.dot(
        pick_ref[...], a_ref[...], preferred_element_type=jnp.float32
    ).astype(o_ref.dtype)


def reorder_pair_kernel(pick_ref, k_ref, v_ref, o_ref):
    width = k_ref.shape[1]
    pick = pick_ref[...]
    for index, ref in enumerate((k_ref, v_ref)):
        o_ref[:, index * width : (index + 1) * width] = jnp.dot(
            pick, ref[...], preferred_element_type=jnp.float32
        ).astype(o_ref.dtype)


def reorder(pick, data):
    rows, width = data.shape
    step = 512 if width % 512 == 0 else HD
    return pl.pallas_call(
        reorder_kernel,
        grid=(width // step,),
        in_specs=[
            pl.BlockSpec((rows, rows), lambda i: (0, 0)),
            pl.BlockSpec((rows, step), lambda i: (0, i)),
        ],
        out_specs=pl.BlockSpec((rows, step), lambda i: (0, i)),
        out_shape=jax.ShapeDtypeStruct((rows, width), data.dtype),
        cost_estimate=pl.CostEstimate(
            flops=2 * rows * rows * width, bytes_accessed=4 * rows * width, transcendentals=0
        ),
        name="reorder",
    )(pick, data)


def reorder_pair(pick, key, value, chunk, step):
    rows = key.shape[0]
    return pl.pallas_call(
        reorder_pair_kernel,
        grid=(1,),
        in_specs=[
            pl.BlockSpec((rows, rows), lambda i: (0, 0)),
            pl.BlockSpec((rows, step), lambda i: (0, chunk)),
            pl.BlockSpec((rows, step), lambda i: (0, chunk)),
        ],
        out_specs=pl.BlockSpec((rows, 2 * step), lambda i: (0, 0)),
        out_shape=jax.ShapeDtypeStruct((rows, 2 * step), key.dtype),
        cost_estimate=pl.CostEstimate(
            flops=4 * rows * rows * step, bytes_accessed=8 * rows * step, transcendentals=0
        ),
        name="reorder_pair",
    )(pick, key, value)


def attend_kernel(tile_tok, q_ref, *refs):
    k_refs, v_refs = refs[0:3], refs[3:6]
    bias_ref, back_ref, own_ref, other_ref, att_ref = refs[6:]
    rows = q_ref.shape[0]
    half = rows // 2
    factor = HD ** (-0.5) * math.log2(math.e)
    dims = (((1,), (1,)), ((), ()))
    for tile in range(rows // tile_tok):
        part_q = q_ref[tile * tile_tok : (tile + 1) * tile_tok, :]
        scores = [
            lax.dot_general(part_q, k_ref[...], dims, preferred_element_type=jnp.float32) * factor
            + bias_ref[tile : tile + 1, index * rows : (index + 1) * rows]
            for index, k_ref in enumerate(k_refs)
        ]
        top = functools.reduce(
            jnp.maximum, [jnp.max(part, axis=1, keepdims=True) for part in scores]
        )
        total = 0.0
        denom = 0.0
        for part, v_ref in zip(scores, v_refs):
            expon = jnp.exp2(part - top)
            denom = denom + jnp.sum(expon, axis=1, keepdims=True)
            total = total + jnp.dot(
                expon.astype(jnp.bfloat16), v_ref[...], preferred_element_type=jnp.float32
            )
        att_ref[tile * tile_tok : (tile + 1) * tile_tok, :] = (total / denom).astype(jnp.bfloat16)
    att = att_ref[...]
    own_ref[...] = jnp.dot(
        back_ref[:half, :], att, preferred_element_type=jnp.float32
    ).astype(jnp.bfloat16)
    other_ref[...] = jnp.dot(
        back_ref[half:, :], att, preferred_element_type=jnp.float32
    ).astype(jnp.bfloat16)


def attend(queries, pairs, bias, back, chunk, tile_tok):
    rows = queries.shape[0]
    heads = pairs[0].shape[1] // (2 * HD)
    column = lambda i: (0, i)
    later = lambda i: (0, heads + i)
    whole = lambda i: (0, 0)
    in_specs = [pl.BlockSpec((rows, HD), lambda i: (0, chunk * heads + i))]
    in_specs += [pl.BlockSpec((rows, HD), column)] * 3
    in_specs += [pl.BlockSpec((rows, HD), later)] * 3
    in_specs += [pl.BlockSpec(bias.shape, whole), pl.BlockSpec(back.shape, whole)]
    half = jax.ShapeDtypeStruct((rows // 2, heads * HD), queries.dtype)
    return pl.pallas_call(
        functools.partial(attend_kernel, tile_tok),
        grid=(heads,),
        in_specs=in_specs,
        out_specs=[pl.BlockSpec((rows // 2, HD), column)] * 2,
        out_shape=[half, half],
        scratch_shapes=[pltpu.VMEM((rows, HD), jnp.bfloat16)],
        compiler_params=pltpu.CompilerParams(vmem_limit_bytes=48 << 20),
        cost_estimate=pl.CostEstimate(
            flops=4 * heads * rows * 3 * rows * HD * 2,
            bytes_accessed=16 * rows * heads * HD,
            transcendentals=heads * rows * 3 * rows,
        ),
        name="attend",
    )(queries, *pairs, *pairs, bias, back)


def project_kernel(count, *refs):
    pieces, (own_ref, other_ref, out_ref, all_ref) = refs[: 2 * count], refs[2 * count :]
    step = pieces[0].shape[1]
    depth = own_ref.shape[1]

    @pl.when(pl.program_id(0) == 0)
    def _():
        for index, piece in enumerate(pieces):
            all_ref[:, index * step : (index + 1) * step] = piece[...]

    width = own_ref.shape[2]
    for block in range(own_ref.shape[0]):
        total = jnp.dot(all_ref[:, :depth], own_ref[block], preferred_element_type=jnp.float32)
        total += jnp.dot(all_ref[:, depth:], other_ref[block], preferred_element_type=jnp.float32)
        out_ref[:, block * width : (block + 1) * width] = total.astype(out_ref.dtype)


def project(own, other, weight_own, weight_other):
    count = len(own)
    rows, step = own[0].shape
    blocks, depth, width = weight_own.shape
    group = 1 if width % 128 == 0 else 2
    whole = lambda i: (0, 0)
    each = lambda i: (i, 0, 0)
    return pl.pallas_call(
        functools.partial(project_kernel, count),
        grid=(blocks // group,),
        in_specs=[pl.BlockSpec((rows, step), whole)] * (2 * count)
        + [pl.BlockSpec((group, depth, width), each)] * 2,
        out_specs=pl.BlockSpec((rows, group * width), lambda i: (0, i)),
        out_shape=jax.ShapeDtypeStruct((rows, blocks * width), jnp.bfloat16),
        scratch_shapes=[pltpu.VMEM((rows, 2 * depth), jnp.bfloat16)],
        compiler_params=pltpu.CompilerParams(vmem_limit_bytes=48 << 20),
        cost_estimate=pl.CostEstimate(
            flops=4 * rows * depth * blocks * width,
            bytes_accessed=4 * depth * blocks * width,
            transcendentals=0,
        ),
        name="project",
    )(*own, *other, weight_own, weight_other)


def on_device(query, key, value, tile_mask, order, out_weight):
    slab = order.shape[1]
    tile_tok = slab // tile_mask.shape[1]
    width = query.shape[1]
    step = CHUNK_HEADS * HD
    count = lax.axis_size("tm")
    me = lax.axis_index("tm")
    side = lax.axis_index("head")
    even = me % 2 == 0

    beside = [(i, i ^ 1) for i in range(count)]
    onward = [(i, i + 2) for i in range(0, count - 2, 2)]
    onward += [(i, i - 2) for i in range(3, count, 2)]
    across = [(0, 1), (1, 0)]

    depth = out_weight.shape[0] // 2
    rows_own = lax.dynamic_slice_in_dim(out_weight, side * depth, depth, 0)
    weight_own = lax.all_gather(rows_own, "tm", axis=0, tiled=False)
    weight_other = lax.ppermute(weight_own, "head", across)

    places = jnp.arange(slab, dtype=jnp.int32)
    pick = (order[0][:, None] == places[None, :]).astype(jnp.bfloat16)
    half = slab // 2
    targets = (places + side * half) % slab
    back = (targets[:, None] == order[0][None, :]).astype(jnp.bfloat16)

    low, mid, high = allowed_tiles(tile_mask[0], me, count)
    seen = jnp.concatenate([mid, jnp.where(even, high, low), jnp.where(even, low, high)], axis=1)
    bias = jnp.repeat(jnp.where(seen, 0.0, HIDDEN).astype(jnp.float32), tile_tok, axis=1)

    chunks = range(width // step)
    mine = [reorder_pair(pick, key, value, chunk, step) for chunk in chunks]
    near = [lax.ppermute(pair, "tm", beside) for pair in mine]
    far = [lax.ppermute(pair, "tm", onward) for pair in near]
    queries = reorder(pick, query)

    own, other = [], []
    for chunk in chunks:
        kept, sent = attend(
            queries, (mine[chunk], near[chunk], far[chunk]), bias, back, chunk, tile_tok
        )
        own.append(kept)
        other.append(lax.ppermute(sent, "head", across))
    return project(own, other, weight_own, weight_other)


def solution(mesh):
    placed = (
        P(("clips", "tm"), "head"),
        P(("clips", "tm"), "head"),
        P(("clips", "tm"), "head"),
        P(("clips", "tm"), None, None),
        P(("clips", "tm"), None),
        P(None, "tm"),
    )
    return jax.shard_map(
        on_device,
        mesh=mesh,
        in_specs=placed,
        out_specs=P(("clips", "tm", "head"), None),
        check_vma=False,
    )
```

time: 641 us -> 346 us (0.54)
  waiting for transfers between devices: 400 us -> 209 us
  local copies, waits for them, and re-layouts: 105 us -> 5.56 us
  Pallas kernels: 0 us -> 91.8 us
  matrix products: 77 us -> 0 us
  other arithmetic: 28.2 us -> 2.19 us
  starting transfers between devices: 8.57 us -> 22 us
  blocking collectives: 6.54 us -> 0 us
    ppermute x2 -> x19, waiting for transfers between devices: 399 us -> 68.1 us  [the longest x6 60.8 us: on_device(): near = [lax.ppermute(pair, 'tm', beside) for pair in mine]]
    all_gather x1, waiting for transfers between devices: 0.01 us -> 141 us  [on_device(): weight_own = lax.all_gather(rows_own, 'tm', axis=0, tiled=False)]
    pallas_call x0 -> x14, Pallas kernels: none -> 91.8 us  [the longest x6 52.5 us: attend(): pl.pallas_call(functools.partial(attend_kernel, tile_tok), grid=(heads,),...]
    dot_general x25 -> x0, matrix products: 77 us -> none  [the longest x12 36.5 us: one_head(): jnp.dot(part_q, part_k.T, preferred_element_type=jnp.float32) * scale]
    another operation x4 -> x0, local copies, waits for them, and re-layouts: 31.5 us -> none  [the longest x1 13.6 us: attend(): head_values = values.reshape(3 * rows, heads, HD).transpose(1, 0, 2)]
    while x2 -> x0, local copies, waits for them, and re-layouts: 16.8 us -> none  [attend(): outputs = lax.map(one_head, (head_queries, head_keys, head_values))]
    gather x3 -> x0, local copies, waits for them, and re-layouts: 15.7 us -> none  [to_tiles(): return jnp.take_along_axis(blocks, order[:, :, None], axis=1)]
    ppermute x2 -> x19, starting transfers between devices: 8.56 us -> 22 us  [the longest x6 15.4 us: on_device(): far = [lax.ppermute(pair, 'tm', onward) for pair in near]]
  transfers between devices with their start and end apart: 3 -> 20, of which waited for: 1 -> 9; matrix products, arithmetic and copies ran while one was open for 31% -> 1% of each run, Pallas kernels for 0% -> 22%
where the time goes in v1:
time: 346 us; the launch traced here: 344 us
  waiting for transfers between devices  209 us (60%)
  Pallas kernels  91.8 us (27%)
  starting transfers between devices  22 us (6%)
  between operations  13.6 us (4%)
  local copies, waits for them, and re-layouts  5.56 us (2%)
    all_gather x1, waiting for transfers between devices, on_device(): weight_own = lax.all_gather(rows_own, 'tm', axis=0, tiled=False)  141 us
    ppermute x6, waiting for transfers between devices, on_device(): near = [lax.ppermute(pair, 'tm', beside) for pair in mine]  60.8 us
    pallas_call x6, Pallas kernels, attend(): pl.pallas_call(functools.partial(attend_kernel, tile_tok), grid=(heads,),...  52.5 us
    pallas_call x6, Pallas kernels, reorder_pair(): pl.pallas_call(reorder_pair_kernel, grid=(1,), in_specs=[pl.BlockSpec((ro...  18.9 us
    ppermute x6, starting transfers between devices, on_device(): far = [lax.ppermute(pair, 'tm', onward) for pair in near]  15.4 us
    pallas_call x1, Pallas kernels, project(): pl.pallas_call(functools.partial(project_kernel, count), grid=(blocks //...  15 us
  transfers between devices with their start and end apart: 20, of which 9 were waited for; matrix products, arithmetic and copies ran while one was open for 1% of the time, Pallas kernels for 22%

profile of v1, /device:TPU:0, one launch (start us, length us, event | category | flops | bytes accessed | tf_op | source)
XLA Modules:
  0.0 344.3 jit_solution(16447776036407831356)
XLA Ops:
  6.5 1.7 copy-done
  8.2 1.1 constant_dynamic-slice_fusion
  9.4 141.0 %all-gather.3.cloned.1.call-done = bf16[12288,384]{1,0:T(8,128)(2,1)} async-done(((bf16[1536,384]{1,0:T(8,128)(2,1)}), bf16[12288,384]{1,0:T(8,128)(2,1)}) %all-gather.3.cloned.1.call-update) | async-done | bytes 9437200 | tf_op jit(solution)/shard_map/all_gather | solution.py:215
  150.4 1.5 compare_convert_fusion
  151.8 3.1 reorder_pair.11.refs_0_.refs_3_
  155.0 0.6 collective-permute-start.10
  155.5 3.1 reorder_pair.10.refs_0_.refs_3_
  158.7 1.5 collective-permute-start.8
  160.1 3.2 reorder_pair.9.refs_0_.refs_3_
  163.3 0.6 collective-permute-start.6
  163.9 3.2 reorder_pair.8.refs_0_.refs_3_
  167.1 1.5 collective-permute-start.4
  168.6 3.1 reorder_pair.7.refs_0_.refs_3_
  171.7 0.1 fusion.11
  171.8 0.5 select_reduce_fusion.2
  172.2 3.4 collective-permute-done.10.refs_1_.refs_4_
  175.6 0.6 collective-permute-start.2
  176.2 0.1 broadcast_select_fusion.1
  176.3 16.2 %collective-permute-done.8.refs_1_.refs_4_ = bf16[768,512]{1,0:T(8,128)(2,1)} collective-permute-done((bf16[768,512]{1,0:T(8,128)(2,1)}, bf16[768,512]{1,0:T(8,128)(2,1)}, u32[]{:S(2)}, u32[]{:S(2)}) %collective-permute-start.8) | collective-permute-done | bytes 786464 | tf_op jit(solution)/shard_map/ppermute | solution.py:230
  192.5 2.4 collective-permute-start.11
  194.9 3.1 reorder_pair.6.refs_0_.refs_3_
  198.0 11.3 %collective-permute-done.6.refs_1_.refs_4_ = bf16[768,512]{1,0:T(8,128)(2,1)} collective-permute-done((bf16[768,512]{1,0:T(8,128)(2,1)}, bf16[768,512]{1,0:T(8,128)(2,1)}, u32[]{:S(2)}, u32[]{:S(2)}) %collective-permute-start.6) | collective-permute-done | bytes 786464 | tf_op jit(solution)/shard_map/ppermute | solution.py:230
  209.3 0.6 collective-permute-start
  209.9 16.3 %collective-permute-done.4.refs_1_.refs_4_ = bf16[768,512]{1,0:T(8,128)(2,1)} collective-permute-done((bf16[768,512]{1,0:T(8,128)(2,1)}, bf16[768,512]{1,0:T(8,128)(2,1)}, u32[]{:S(2)}, u32[]{:S(2)}) %collective-permute-start.4) | collective-permute-done | bytes 786464 | tf_op jit(solution)/shard_map/ppermute | solution.py:230
  226.2 2.4 collective-permute-start.9
  228.8 0.7 copy.11
  229.4 13.6 %collective-permute-done.2.refs_1_.refs_4_ = bf16[768,512]{1,0:T(8,128)(2,1)} collective-permute-done((bf16[768,512]{1,0:T(8,128)(2,1)}, bf16[768,512]{1,0:T(8,128)(2,1)}, u32[]{:S(2)}, u32[]{:S(2)}) %collective-permute-start.2) | collective-permute-done | bytes 786464 | tf_op jit(solution)/shard_map/ppermute | solution.py:230
  243.0 2.5 collective-permute-start.7
  245.5 5.4 %reorder.1.q_ref = bf16[768,1536]{1,0:T(8,128)(2,1)} custom-call(bf16[768,768]{1,0:T(8,128)(2,1)} %get-tuple-element.36.pick_ref, bf16[768,1536]{1,0:T(8,128)(2,1)} %a_ref.1), custom_call_target="tpu_custom_call" | custom-call | flops 1811939328 | bytes 4718592 | tf_op jit(solution)/shard_map/reorder/pallas_call | solution.py:58
  250.9 3.5 %collective-permute-start.5 = (bf16[768,512]{1,0:T(8,128)(2,1)}, bf16[768,512]{1,0:T(8,128)(2,1)S(1)}, u32[]{:S(2)}, u32[]{:S(2)}) collective-permute-start(bf16[768,512]{1,0:T(8,128)(2,1)} %collective-permute-done.4.refs_1_.refs_4_), channel_id=1, source_target_pairs={{0,4},{4,8},{8,12},{6,2},{10,6},{14,10},{1,5},{5,9},{9,13},{7,3},{... | collective-permute-start | bytes 2359304 | tf_op jit(solution)/shard_map/ppermute | solution.py:231
  254.4 1.1 copy-done.4
  255.5 0.9 copy-done.7
  256.4 8.8 %attend.11 = (bf16[384,256]{1,0:T(8,128)(2,1)S(1)}, bf16[384,256]{1,0:T(8,128)(2,1)S(1)}) custom-call(bf16[768,1536]{1,0:T(8,128)(2,1)} %reorder.1.q_ref, bf16[768,512]{1,0:T(8,128)(2,1)S(1)} %copy-done.4, bf16[768,512]{1,0:T(8,128)(2,1)} %collective-permute-done.10.refs_1_.refs_4_, bf16[768,512]{1,0:T(8,128)(2,1)} %collective-permute-done.11.refs_2_.refs_5_, ...), custom_call_target="tpu_custom_call" | custom-call | flops 3623878656 | bytes 3145728 | tf_op jit(solution)/shard_map/attend/pallas_call | solution.py:139
  265.2 2.5 collective-permute-start.3
  267.8 2.1 collective-permute-start.1
  269.9 8.8 %attend.10 = (bf16[384,256]{1,0:T(8,128)(2,1)S(1)}, bf16[384,256]{1,0:T(8,128)(2,1)S(1)}) custom-call(bf16[768,1536]{1,0:T(8,128)(2,1)} %reorder.1.q_ref, bf16[768,512]{1,0:T(8,128)(2,1)S(1)} %copy-done.3, bf16[768,512]{1,0:T(8,128)(2,1)} %collective-permute-done.8.refs_1_.refs_4_, bf16[768,512]{1,0:T(8,128)(2,1)} %collective-permute-done.9.refs_2_.refs_5_, ...), custom_call_target="tpu_custom_call" | custom-call | flops 3623878656 | bytes 3145728 | tf_op jit(solution)/shard_map/attend/pallas_call | solution.py:139
  278.9 8.9 %attend.9 = (bf16[384,256]{1,0:T(8,128)(2,1)S(1)}, bf16[384,256]{1,0:T(8,128)(2,1)S(1)}) custom-call(bf16[768,1536]{1,0:T(8,128)(2,1)} %reorder.1.q_ref, bf16[768,512]{1,0:T(8,128)(2,1)S(1)} %copy-done.2, bf16[768,512]{1,0:T(8,128)(2,1)} %collective-permute-done.6.refs_1_.refs_4_, bf16[768,512]{1,0:T(8,128)(2,1)} %collective-permute-done.7.refs_2_.refs_5_, ...), custom_call_target="tpu_custom_call" | custom-call | flops 3623878656 | bytes 3145728 | tf_op jit(solution)/shard_map/attend/pallas_call | solution.py:139
  287.8 0.5 collective-permute-start.16
  288.2 8.6 %attend.8 = (bf16[384,256]{1,0:T(8,128)(2,1)S(1)}, bf16[384,256]{1,0:T(8,128)(2,1)S(1)}) custom-call(bf16[768,1536]{1,0:T(8,128)(2,1)} %reorder.1.q_ref, bf16[768,512]{1,0:T(8,128)(2,1)S(1)} %copy-done.1, bf16[768,512]{1,0:T(8,128)(2,1)} %collective-permute-done.4.refs_1_.refs_4_, bf16[768,512]{1,0:T(8,128)(2,1)S(1)} %collective-permute-done.5.refs_2_.refs_5_, ...), custom_call_target="tpu_custom_call" | custom-call | flops 3623878656 | bytes 3145728 | tf_op jit(solution)/shard_map/attend/pallas_call | solution.py:139
  296.9 0.2 collective-permute-start.15
  297.1 8.7 %attend.7 = (bf16[384,256]{1,0:T(8,128)(2,1)S(1)}, bf16[384,256]{1,0:T(8,128)(2,1)S(1)}) custom-call(bf16[768,1536]{1,0:T(8,128)(2,1)} %reorder.1.q_ref, bf16[768,512]{1,0:T(8,128)(2,1)S(1)} %copy-done.5, bf16[768,512]{1,0:T(8,128)(2,1)} %collective-permute-done.2.refs_1_.refs_4_, bf16[768,512]{1,0:T(8,128)(2,1)S(1)} %collective-permute-done.3.refs_2_.refs_5_, ...), custom_call_target="tpu_custom_call" | custom-call | flops 3623878656 | bytes 3145728 | tf_op jit(solution)/shard_map/attend/pallas_call | solution.py:139
  305.8 6.0 %collective-permute-done.1.refs_2_.refs_5_ = bf16[768,512]{1,0:T(8,128)(2,1)S(1)} collective-permute-done((bf16[768,512]{1,0:T(8,128)(2,1)}, bf16[768,512]{1,0:T(8,128)(2,1)S(1)}, u32[]{:S(2)}, u32[]{:S(2)}) %collective-permute-start.1) | collective-permute-done | bytes 786464 | tf_op jit(solution)/shard_map/ppermute | solution.py:231
  311.8 8.6 %attend.6 = (bf16[384,256]{1,0:T(8,128)(2,1)S(1)}, bf16[384,256]{1,0:T(8,128)(2,1)S(1)}) custom-call(bf16[768,1536]{1,0:T(8,128)(2,1)} %reorder.1.q_ref, bf16[768,512]{1,0:T(8,128)(2,1)S(1)} %copy-done.6, bf16[768,512]{1,0:T(8,128)(2,1)} %collective-permute-done.refs_1_.refs_4_, bf16[768,512]{1,0:T(8,128)(2,1)S(1)} %collective-permute-done.1.refs_2_.refs_5_, ...), custom_call_target="tpu_custom_call" | custom-call | flops 3623878656 | bytes 3145728 | tf_op jit(solution)/shard_map/attend/pallas_call | solution.py:139
  320.4 0.6 collective-permute-start.13
  321.0 0.1 collective-permute-start.12
  321.1 1.0 collective-permute-done.13.refs_7_
  322.0 0.4 collective-permute-done.12.refs_6_
  322.4 15.0 %project.1 = bf16[384,3072]{1,0:T(8,128)(2,1)} custom-call(bf16[384,256]{1,0:T(8,128)(2,1)S(1)} %get-tuple-element.17.refs_0_, bf16[384,256]{1,0:T(8,128)(2,1)S(1)} %get-tuple-element.18.refs_1_, bf16[384,256]{1,0:T(8,128)(2,1)S(1)} %get-tuple-element.19.refs_2_, bf16[384,256]{1,0:T(8,128)(2,1)S(1)} %get-tuple-element.20.refs_3_, ...), custom_call_target="tpu_custom_call" | custom-call | flops 7247757312 | bytes 18874368 | tf_op jit(solution)/shard_map/project/pallas_call | solution.py:180
  (42 shorter events, 0.4 us)
Async XLA Ops:
  6.5 1.7 copy-start
  6.5 143.8 %copy-start.10 = (s32[1,768]{1,0:T(1,128)S(1)}, s32[1,768]{1,0:T(1,128)}, u32[]{:S(2)}) copy-start(s32[1,768]{1,0:T(1,128)} %param.10) | copy-start | bytes 9220
  6.5 143.8 %all-gather.3.cloned.1.call-start = ((), (), s32[]{:S(2)}) async-start(), calls=%async_computation | async-start | bytes 10616832 | tf_op jit(solution)/shard_map/all_gather | solution.py:215
  150.3 172.1 %collective-permute-start.18 = (bf16[8,1536,384]{2,1,0:T(8,128)(2,1)}, bf16[8,1536,384]{2,1,0:T(8,128)(2,1)}, u32[]{:S(2)}, u32[]{:S(2)}) collective-permute-start(bf16[8,1536,384]{2,1,0:T(8,128)(2,1)} %bitcast.16), channel_id=1, source_target_pairs={{0,1},{1,0},{2,3},{3,2},{4,5},{5,4},{6,7},{7,6},{8,9},{9,8},{10,11... | collective-permute-start | bytes 28311560 | tf_op jit(solution)/shard_map/ppermute | solution.py:216
  155.0 20.7 %collective-permute-start.10 = (bf16[768,512]{1,0:T(8,128)(2,1)}, bf16[768,512]{1,0:T(8,128)(2,1)}, u32[]{:S(2)}, u32[]{:S(2)}) collective-permute-start(bf16[768,512]{1,0:T(8,128)(2,1)} %reorder_pair.11.refs_0_.refs_3_), channel_id=1, source_target_pairs={{0,2},{2,0},{4,6},{6,4},{8,10},{10,8},{12,14},{14,12},{1,3},{3,1},... | collective-permute-start | bytes 2359304 | tf_op jit(solution)/shard_map/ppermute | solution.py:230
  158.7 33.8 %collective-permute-start.8 = (bf16[768,512]{1,0:T(8,128)(2,1)}, bf16[768,512]{1,0:T(8,128)(2,1)}, u32[]{:S(2)}, u32[]{:S(2)}) collective-permute-start(bf16[768,512]{1,0:T(8,128)(2,1)} %reorder_pair.10.refs_0_.refs_3_), channel_id=1, source_target_pairs={{0,2},{2,0},{4,6},{6,4},{8,10},{10,8},{12,14},{14,12},{1,3},{3,1},... | collective-permute-start | bytes 2359304 | tf_op jit(solution)/shard_map/ppermute | solution.py:230
  163.3 5.2 %copy-start.9 = (s32[1,6,27]{2,0,1:T(1,128)S(1)}, s32[1,6,27]{2,0,1:T(1,128)}, u32[]{:S(2)}) copy-start(s32[1,6,27]{2,0,1:T(1,128)} %param.9) | copy-start | bytes 1948
  163.3 46.0 %collective-permute-start.6 = (bf16[768,512]{1,0:T(8,128)(2,1)}, bf16[768,512]{1,0:T(8,128)(2,1)}, u32[]{:S(2)}, u32[]{:S(2)}) collective-permute-start(bf16[768,512]{1,0:T(8,128)(2,1)} %reorder_pair.9.refs_0_.refs_3_), channel_id=1, source_target_pairs={{0,2},{2,0},{4,6},{6,4},{8,10},{10,8},{12,14},{14,12},{1,3},{3,1},... | collective-permute-start | bytes 2359304 | tf_op jit(solution)/shard_map/ppermute | solution.py:230
  167.1 59.1 %collective-permute-start.4 = (bf16[768,512]{1,0:T(8,128)(2,1)}, bf16[768,512]{1,0:T(8,128)(2,1)}, u32[]{:S(2)}, u32[]{:S(2)}) collective-permute-start(bf16[768,512]{1,0:T(8,128)(2,1)} %reorder_pair.8.refs_0_.refs_3_), channel_id=1, source_target_pairs={{0,2},{2,0},{4,6},{6,4},{8,10},{10,8},{12,14},{14,12},{1,3},{3,1},... | collective-permute-start | bytes 2359304 | tf_op jit(solution)/shard_map/ppermute | solution.py:230
  175.6 67.4 %collective-permute-start.2 = (bf16[768,512]{1,0:T(8,128)(2,1)}, bf16[768,512]{1,0:T(8,128)(2,1)}, u32[]{:S(2)}, u32[]{:S(2)}) collective-permute-start(bf16[768,512]{1,0:T(8,128)(2,1)} %reorder_pair.7.refs_0_.refs_3_), channel_id=1, source_target_pairs={{0,2},{2,0},{4,6},{6,4},{8,10},{10,8},{12,14},{14,12},{1,3},{3,1},... | collective-permute-start | bytes 2359304 | tf_op jit(solution)/shard_map/ppermute | solution.py:230
  192.5 58.4 %collective-permute-start.11 = (bf16[768,512]{1,0:T(8,128)(2,1)}, bf16[768,512]{1,0:T(8,128)(2,1)}, u32[]{:S(2)}, u32[]{:S(2)}) collective-permute-start(bf16[768,512]{1,0:T(8,128)(2,1)} %collective-permute-done.10.refs_1_.refs_4_), channel_id=1, source_target_pairs={{0,4},{4,8},{8,12},{6,2},{10,6},{14,10},{1,5},{5,9},{9,13},{7,3},{... | collective-permute-start | bytes 2359304 | tf_op jit(solution)/shard_map/ppermute | solution.py:231
  209.3 55.9 %collective-permute-start = (bf16[768,512]{1,0:T(8,128)(2,1)}, bf16[768,512]{1,0:T(8,128)(2,1)}, u32[]{:S(2)}, u32[]{:S(2)}) collective-permute-start(bf16[768,512]{1,0:T(8,128)(2,1)} %reorder_pair.6.refs_0_.refs_3_), channel_id=1, source_target_pairs={{0,2},{2,0},{4,6},{6,4},{8,10},{10,8},{12,14},{14,12},{1,3},{3,1},... | collective-permute-start | bytes 2359304 | tf_op jit(solution)/shard_map/ppermute | solution.py:230
  226.2 41.6 %collective-permute-start.9 = (bf16[768,512]{1,0:T(8,128)(2,1)}, bf16[768,512]{1,0:T(8,128)(2,1)}, u32[]{:S(2)}, u32[]{:S(2)}) collective-permute-start(bf16[768,512]{1,0:T(8,128)(2,1)} %collective-permute-done.8.refs_1_.refs_4_), channel_id=1, source_target_pairs={{0,4},{4,8},{8,12},{6,2},{10,6},{14,10},{1,5},{5,9},{9,13},{7,3},{... | collective-permute-start | bytes 2359304 | tf_op jit(solution)/shard_map/ppermute | solution.py:231
  243.0 35.7 %collective-permute-start.7 = (bf16[768,512]{1,0:T(8,128)(2,1)}, bf16[768,512]{1,0:T(8,128)(2,1)}, u32[]{:S(2)}, u32[]{:S(2)}) collective-permute-start(bf16[768,512]{1,0:T(8,128)(2,1)} %collective-permute-done.6.refs_1_.refs_4_), channel_id=1, source_target_pairs={{0,4},{4,8},{8,12},{6,2},{10,6},{14,10},{1,5},{5,9},{9,13},{7,3},{... | collective-permute-start | bytes 2359304 | tf_op jit(solution)/shard_map/ppermute | solution.py:231
  250.9 36.9 %collective-permute-start.5 = (bf16[768,512]{1,0:T(8,128)(2,1)}, bf16[768,512]{1,0:T(8,128)(2,1)S(1)}, u32[]{:S(2)}, u32[]{:S(2)}) collective-permute-start(bf16[768,512]{1,0:T(8,128)(2,1)} %collective-permute-done.4.refs_1_.refs_4_), channel_id=1, source_target_pairs={{0,4},{4,8},{8,12},{6,2},{10,6},{14,10},{1,5},{5,9},{9,13},{7,3},{... | collective-permute-start | bytes 2359304 | tf_op jit(solution)/shard_map/ppermute | solution.py:231
  254.4 1.1 copy-start.4
  255.5 0.9 copy-start.7
  256.4 13.5 %copy-start.3 = (bf16[768,512]{1,0:T(8,128)(2,1)S(1)}, bf16[768,512]{1,0:T(8,128)(2,1)}, u32[]{:S(2)}) copy-start(bf16[768,512]{1,0:T(8,128)(2,1)} %reorder_pair.10.refs_0_.refs_3_) | copy-start | bytes 2359300
  265.2 13.6 %copy-start.2 = (bf16[768,512]{1,0:T(8,128)(2,1)S(1)}, bf16[768,512]{1,0:T(8,128)(2,1)}, u32[]{:S(2)}) copy-start(bf16[768,512]{1,0:T(8,128)(2,1)} %reorder_pair.9.refs_0_.refs_3_) | copy-start | bytes 2359300
  265.2 31.6 %collective-permute-start.3 = (bf16[768,512]{1,0:T(8,128)(2,1)}, bf16[768,512]{1,0:T(8,128)(2,1)S(1)}, u32[]{:S(2)}, u32[]{:S(2)}) collective-permute-start(bf16[768,512]{1,0:T(8,128)(2,1)} %collective-permute-done.2.refs_1_.refs_4_), channel_id=1, source_target_pairs={{0,4},{4,8},{8,12},{6,2},{10,6},{14,10},{1,5},{5,9},{9,13},{7,3},{... | collective-permute-start | bytes 2359304 | tf_op jit(solution)/shard_map/ppermute | solution.py:231
  267.8 44.0 %collective-permute-start.1 = (bf16[768,512]{1,0:T(8,128)(2,1)}, bf16[768,512]{1,0:T(8,128)(2,1)S(1)}, u32[]{:S(2)}, u32[]{:S(2)}) collective-permute-start(bf16[768,512]{1,0:T(8,128)(2,1)} %collective-permute-done.refs_1_.refs_4_), channel_id=1, source_target_pairs={{0,4},{4,8},{8,12},{6,2},{10,6},{14,10},{1,5},{5,9},{9,13},{7,3},{... | collective-permute-start | bytes 2359304 | tf_op jit(solution)/shard_map/ppermute | solution.py:231
  278.7 9.5 %copy-start.1 = (bf16[768,512]{1,0:T(8,128)(2,1)S(1)}, bf16[768,512]{1,0:T(8,128)(2,1)}, u32[]{:S(2)}) copy-start(bf16[768,512]{1,0:T(8,128)(2,1)} %reorder_pair.8.refs_0_.refs_3_) | copy-start | bytes 2359300
  278.8 9.5 %copy-start.8 = (f32[1,6,18,128]{3,1,2,0:T(8,128)S(1)}, f32[1,6,18,128]{3,1,2,0:T(8,128)}, u32[]{:S(2)}) copy-start(f32[1,6,18,128]{3,1,2,0:T(8,128)} %copy.11) | copy-start | bytes 165892
  278.8 41.6 %collective-permute-start.17 = (bf16[384,256]{1,0:T(8,128)(2,1)S(1)}, bf16[384,256]{1,0:T(8,128)(2,1)S(1)}, u32[]{:S(2)}, u32[]{:S(2)}) collective-permute-start(bf16[384,256]{1,0:T(8,128)(2,1)S(1)} %get-tuple-element.28), channel_id=1, source_target_pairs={{0,1},{1,0},{2,3},{3,2},{4,5},{5,4},{6,7},{7,6},{8,9},{9,8},{10,11... | collective-permute-start | bytes 589832 | tf_op jit(solution)/shard_map/ppermute | solution.py:240
  287.7 9.3 %copy-start.5 = (bf16[768,512]{1,0:T(8,128)(2,1)S(1)}, bf16[768,512]{1,0:T(8,128)(2,1)}, u32[]{:S(2)}) copy-start(bf16[768,512]{1,0:T(8,128)(2,1)} %reorder_pair.7.refs_0_.refs_3_) | copy-start | bytes 2359300
  287.8 33.2 %collective-permute-start.16 = (bf16[384,256]{1,0:T(8,128)(2,1)S(1)}, bf16[384,256]{1,0:T(8,128)(2,1)S(1)}, u32[]{:S(2)}, u32[]{:S(2)}) collective-permute-start(bf16[384,256]{1,0:T(8,128)(2,1)S(1)} %get-tuple-element.27), channel_id=1, source_target_pairs={{0,1},{1,0},{2,3},{3,2},{4,5},{5,4},{6,7},{7,6},{8,9},{9,8},{10,11... | collective-permute-start | bytes 589832 | tf_op jit(solution)/shard_map/ppermute | solution.py:240
  296.9 14.9 %copy-start.6 = (bf16[768,512]{1,0:T(8,128)(2,1)S(1)}, bf16[768,512]{1,0:T(8,128)(2,1)}, u32[]{:S(2)}) copy-start(bf16[768,512]{1,0:T(8,128)(2,1)} %reorder_pair.6.refs_0_.refs_3_) | copy-start | bytes 2359300
  296.9 24.2 %collective-permute-start.15 = (bf16[384,256]{1,0:T(8,128)(2,1)S(1)}, bf16[384,256]{1,0:T(8,128)(2,1)S(1)}, u32[]{:S(2)}, u32[]{:S(2)}) collective-permute-start(bf16[384,256]{1,0:T(8,128)(2,1)S(1)} %get-tuple-element.26), channel_id=1, source_target_pairs={{0,1},{1,0},{2,3},{3,2},{4,5},{5,4},{6,7},{7,6},{8,9},{9,8},{10,11... | collective-permute-start | bytes 589832 | tf_op jit(solution)/shard_map/ppermute | solution.py:240
  311.8 9.3 %collective-permute-start.14 = (bf16[384,256]{1,0:T(8,128)(2,1)S(1)}, bf16[384,256]{1,0:T(8,128)(2,1)S(1)}, u32[]{:S(2)}, u32[]{:S(2)}) collective-permute-start(bf16[384,256]{1,0:T(8,128)(2,1)S(1)} %get-tuple-element.25), channel_id=1, source_target_pairs={{0,1},{1,0},{2,3},{3,2},{4,5},{5,4},{6,7},{7,6},{8,9},{9,8},{10,11... | collective-permute-start | bytes 589832 | tf_op jit(solution)/shard_map/ppermute | solution.py:240
  320.4 1.6 collective-permute-start.13
  321.0 1.4 collective-permute-start.12
Sparse Core Ops, SparseCore 0:
  9.5 140.7 all-gather.2

commit v2 on v1

--- a/solution.py
+++ b/solution.py
@@ -10,7 +10,8 @@
 
 HD = 128
 GW = 3
-CHUNK_HEADS = 2
+PIECES = 2
+TIES = (1, 3)
 HIDDEN = -1e30
 
 
@@ -97,11 +98,14 @@
     half = rows // 2
     factor = HD ** (-0.5) * math.log2(math.e)
     dims = (((1,), (1,)), ((), ()))
-    for tile in range(rows // tile_tok):
-        part_q = q_ref[tile * tile_tok : (tile + 1) * tile_tok, :]
+
+    @pl.loop(0, rows // tile_tok)
+    def _(tile):
+        place = pl.ds(pl.multiple_of(tile * tile_tok, tile_tok), tile_tok)
+        part_q = q_ref[place, :]
         scores = [
             lax.dot_general(part_q, k_ref[...], dims, preferred_element_type=jnp.float32) * factor
-            + bias_ref[tile : tile + 1, index * rows : (index + 1) * rows]
+            + bias_ref[pl.ds(tile, 1), index * rows : (index + 1) * rows]
             for index, k_ref in enumerate(k_refs)
         ]
         top = functools.reduce(
@@ -115,7 +119,8 @@
             total = total + jnp.dot(
                 expon.astype(jnp.bfloat16), v_ref[...], preferred_element_type=jnp.float32
             )
-        att_ref[tile * tile_tok : (tile + 1) * tile_tok, :] = (total / denom).astype(jnp.bfloat16)
+        att_ref[place, :] = (total / denom).astype(jnp.bfloat16)
+
     att = att_ref[...]
     own_ref[...] = jnp.dot(
         back_ref[:half, :], att, preferred_element_type=jnp.float32
@@ -153,53 +158,60 @@
     )(queries, *pairs, *pairs, bias, back)
 
 
-def project_kernel(count, *refs):
-    pieces, (own_ref, other_ref, out_ref, all_ref) = refs[: 2 * count], refs[2 * count :]
-    step = pieces[0].shape[1]
-    depth = own_ref.shape[1]
+def project_kernel(count, starts, shift_ref, *refs):
+    pieces, weights = refs[: 2 * count], refs[2 * count : -2]
+    out_ref, all_ref = refs[-2:]
+    depth = all_ref.shape[1] // 2
+    part = weights[0].shape[1]
+    width = weights[0].shape[2]
 
     @pl.when(pl.program_id(0) == 0)
     def _():
         for index, piece in enumerate(pieces):
-            all_ref[:, index * step : (index + 1) * step] = piece[...]
-
-    width = own_ref.shape[2]
-    for block in range(own_ref.shape[0]):
-        total = jnp.dot(all_ref[:, :depth], own_ref[block], preferred_element_type=jnp.float32)
-        total += jnp.dot(all_ref[:, depth:], other_ref[block], preferred_element_type=jnp.float32)
+            side, place = index // count, starts[index % count]
+            column = side * depth + lax.rem(place + shift_ref[0], depth)
+            all_ref[:, pl.ds(pl.multiple_of(column, HD), piece.shape[1])] = piece[...]
+
+    for block in range(weights[0].shape[0]):
+        total = 0.0
+        for index, weight in enumerate(weights):
+            total = total + jnp.dot(
+                all_ref[:, index * part : (index + 1) * part],
+                weight[block],
+                preferred_element_type=jnp.float32,
+            )
         out_ref[:, block * width : (block + 1) * width] = total.astype(out_ref.dtype)
 
 
-def project(own, other, weight_own, weight_other):
+def project(own, other, starts, shift, weights):
     count = len(own)
-    rows, step = own[0].shape
-    blocks, depth, width = weight_own.shape
+    rows = own[0].shape[0]
+    blocks, part, width = weights[0].shape
+    depth = part * len(weights)
     group = 1 if width % 128 == 0 else 2
-    whole = lambda i: (0, 0)
-    each = lambda i: (i, 0, 0)
     return pl.pallas_call(
-        functools.partial(project_kernel, count),
+        functools.partial(project_kernel, count, starts),
         grid=(blocks // group,),
-        in_specs=[pl.BlockSpec((rows, step), whole)] * (2 * count)
-        + [pl.BlockSpec((group, depth, width), each)] * 2,
+        in_specs=[pl.BlockSpec(memory_space=pltpu.SMEM)]
+        + [pl.BlockSpec(piece.shape, lambda i: (0, 0)) for piece in own + other]
+        + [pl.BlockSpec((group, part, width), lambda i: (i, 0, 0))] * len(weights),
         out_specs=pl.BlockSpec((rows, group * width), lambda i: (0, i)),
         out_shape=jax.ShapeDtypeStruct((rows, blocks * width), jnp.bfloat16),
-        scratch_shapes=[pltpu.VMEM((rows, 2 * depth), jnp.bfloat16)],
+        scratch_shapes=[pltpu.VMEM((rows, depth), jnp.bfloat16)],
         compiler_params=pltpu.CompilerParams(vmem_limit_bytes=48 << 20),
         cost_estimate=pl.CostEstimate(
-            flops=4 * rows * depth * blocks * width,
-            bytes_accessed=4 * depth * blocks * width,
+            flops=2 * rows * depth * blocks * width,
+            bytes_accessed=2 * depth * blocks * width,
             transcendentals=0,
         ),
         name="project",
-    )(*own, *other, weight_own, weight_other)
+    )(shift, *own, *other, *weights)
 
 
 def on_device(query, key, value, tile_mask, order, out_weight):
     slab = order.shape[1]
     tile_tok = slab // tile_mask.shape[1]
     width = query.shape[1]
-    step = CHUNK_HEADS * HD
     count = lax.axis_size("tm")
     me = lax.axis_index("tm")
     side = lax.axis_index("head")
@@ -210,10 +222,15 @@
     onward += [(i, i - 2) for i in range(3, count, 2)]
     across = [(0, 1), (1, 0)]
 
+    clip = lax.axis_index("clips") % 2
+    paired = [(i, i ^ 1) for i in range(lax.axis_size("clips"))]
     depth = out_weight.shape[0] // 2
-    rows_own = lax.dynamic_slice_in_dim(out_weight, side * depth, depth, 0)
-    weight_own = lax.all_gather(rows_own, "tm", axis=0, tiled=False)
-    weight_other = lax.ppermute(weight_own, "head", across)
+    part = depth // (2 * PIECES)
+    gathered = []
+    for piece in range(PIECES):
+        start = side * depth + clip * (depth // 2) + piece * part
+        rows = lax.dynamic_slice_in_dim(out_weight, start, part, 0)
+        gathered.append(lax.all_gather(rows, "tm", axis=0, tiled=False))
 
     places = jnp.arange(slab, dtype=jnp.int32)
     pick = (order[0][:, None] == places[None, :]).astype(jnp.bfloat16)
@@ -225,20 +242,44 @@
     seen = jnp.concatenate([mid, jnp.where(even, high, low), jnp.where(even, low, high)], axis=1)
     bias = jnp.repeat(jnp.where(seen, 0.0, HIDDEN).astype(jnp.float32), tile_tok, axis=1)
 
-    chunks = range(width // step)
-    mine = [reorder_pair(pick, key, value, chunk, step) for chunk in chunks]
+    heads = width // HD
+    sizes = [2] * (heads // 2 - 1) + [1, 1]
+    starts = [sum(sizes[:index]) for index in range(len(sizes))]
+    chunks = range(len(sizes))
+    mine = []
+    for start, size in zip(starts, sizes):
+        pair = reorder_pair(pick, key, value, start // size, size * HD)
+        pick, pair = lax.optimization_barrier((pick, pair))
+        mine.append(pair)
     near = [lax.ppermute(pair, "tm", beside) for pair in mine]
     far = [lax.ppermute(pair, "tm", onward) for pair in near]
     queries = reorder(pick, query)
 
-    own, other = [], []
+    own, other, crossed = [], [], []
     for chunk in chunks:
+        ahead = min(chunk + 2, len(sizes) - 1)
+        queries, near[ahead] = lax.optimization_barrier((queries, near[ahead]))
+        if chunk == TIES[1] + 2:
+            queries, crossed[0] = lax.optimization_barrier((queries, crossed[0]))
         kept, sent = attend(
-            queries, (mine[chunk], near[chunk], far[chunk]), bias, back, chunk, tile_tok
+            queries,
+            (mine[chunk], near[chunk], far[chunk]),
+            bias,
+            back,
+            starts[chunk] // sizes[chunk],
+            tile_tok,
         )
+        queries, kept = lax.optimization_barrier((queries, kept))
+        if chunk in TIES:
+            piece = TIES.index(chunk)
+            gathered[piece], kept = lax.optimization_barrier((gathered[piece], kept))
+            crossed.append(lax.ppermute(gathered[piece], "clips", paired))
         own.append(kept)
         other.append(lax.ppermute(sent, "head", across))
-    return project(own, other, weight_own, weight_other)
+    weights = gathered + crossed
+    weights = weights + [lax.ppermute(weight, "head", across) for weight in weights]
+    shift = (clip * (depth // 2)).astype(jnp.int32).reshape(1)
+    return project(own, other, [start * HD for start in starts], shift, weights)
 
 
 def solution(mesh):

time: 346 us -> 364 us (1.052)
  Pallas kernels: 91.8 us -> 113 us
  waiting for transfers between devices: 209 us -> 188 us
  starting transfers between devices: 22 us -> 39.4 us
    all_gather x1 -> x2, waiting for transfers between devices: 141 us -> 0.01 us  [on_device(): gathered.append(lax.all_gather(rows, 'tm', axis=0, tiled=False))]
    ppermute x1 -> x6, waiting for transfers between devices: 0.01 us -> 68.7 us  [the longest x2 68.7 us: on_device(): crossed.append(lax.ppermute(gathered[piece], 'clips', paired))]
    ppermute x6 -> x7, waiting for transfers between devices: 5.96 us -> 32.2 us  [on_device(): far = [lax.ppermute(pair, 'tm', onward) for pair in near]]
    ppermute x6 -> x7, waiting for transfers between devices: 60.8 us -> 79.5 us  [on_device(): near = [lax.ppermute(pair, 'tm', beside) for pair in mine]]
    pallas_call x6 -> x7, Pallas kernels: 52.5 us -> 70 us  [attend(): pl.pallas_call(functools.partial(attend_kernel, tile_tok), grid=(heads,),...]
    ppermute x6 -> x7, starting transfers between devices: 15.4 us -> 28.4 us  [on_device(): far = [lax.ppermute(pair, 'tm', onward) for pair in near]]
    ppermute x6 -> x7, waiting for transfers between devices: 1.36 us -> 6.51 us  [on_device(): other.append(lax.ppermute(sent, 'head', across))]
    pallas_call x6 -> x7, Pallas kernels: 18.9 us -> 21.7 us  [reorder_pair(): pl.pallas_call(reorder_pair_kernel, grid=(1,), in_specs=[pl.BlockSpec((ro...]
  transfers between devices with their start and end apart: 20 -> 29, of which waited for: 9 -> 16; matrix products, arithmetic and copies ran while one was open for 1% -> 1% of each run, Pallas kernels for 22% -> 27%
where the time goes in v2:
time: 364 us; the launch traced here: 362 us
  waiting for transfers between devices  188 us (52%)
  Pallas kernels  113 us (31%)
  starting transfers between devices  39.4 us (11%)
  between operations  13.8 us (4%)
  local copies, waits for them, and re-layouts  5.51 us (2%)
    ppermute x7, waiting for transfers between devices, on_device(): near = [lax.ppermute(pair, 'tm', beside) for pair in mine]  79.5 us
    pallas_call x7, Pallas kernels, attend(): pl.pallas_call(functools.partial(attend_kernel, tile_tok), grid=(heads,),...  70 us
    ppermute x2, waiting for transfers between devices, on_device(): crossed.append(lax.ppermute(gathered[piece], 'clips', paired))  68.7 us
    ppermute x7, waiting for transfers between devices, on_device(): far = [lax.ppermute(pair, 'tm', onward) for pair in near]  32.2 us
    ppermute x7, starting transfers between devices, on_device(): far = [lax.ppermute(pair, 'tm', onward) for pair in near]  28.4 us
    pallas_call x7, Pallas kernels, reorder_pair(): pl.pallas_call(reorder_pair_kernel, grid=(1,), in_specs=[pl.BlockSpec((ro...  21.7 us
    pallas_call x1, Pallas kernels, project(): pl.pallas_call(functools.partial(project_kernel, count, starts), grid=(bl...  15.7 us
    ppermute x7, starting transfers between devices, on_device(): near = [lax.ppermute(pair, 'tm', beside) for pair in mine]  7.72 us
  transfers between devices with their start and end apart: 29, of which 16 were waited for; matrix products, arithmetic and copies ran while one was open for 1% of the time, Pallas kernels for 27%

profile of v2, /device:TPU:0, one launch (start us, length us, event | category | flops | bytes accessed | tf_op | source)
XLA Modules:
  0.0 362.0 jit_solution(16714907803928136340)
XLA Ops:
  6.5 1.9 constant_dynamic-slice_fusion
  8.6 0.7 all-gather.7.cloned.1.call-update
  9.3 0.7 reduce
  10.0 1.5 compare_convert_fusion
  11.4 3.1 reorder_pair.7.refs_0_.refs_3_
  14.6 3.1 reorder_pair.8.refs_0_.refs_3_
  17.7 3.3 reorder_pair.9.refs_0_.refs_3_
  21.0 3.0 collective-permute-start
  24.1 3.1 reorder_pair.10.refs_0_.refs_3_
  27.2 1.9 collective-permute-start.3
  29.3 3.2 reorder_pair.11.refs_0_.refs_3_
  32.4 1.9 collective-permute-start.6
  35.0 37.8 %collective-permute-done.1.refs_1_.refs_4_ = bf16[768,512]{1,0:T(8,128)(2,1)} collective-permute-done((bf16[768,512]{1,0:T(8,128)(2,1)S(1)}, bf16[768,512]{1,0:T(8,128)(2,1)}, u32[]{:S(2)}, u32[]{:S(2)}) %collective-permute-start.1) | collective-permute-done | bytes 786464 | tf_op jit(solution)/shard_map/ppermute | solution.py:254
  72.9 4.4 %collective-permute-start.2 = (bf16[768,512]{1,0:T(8,128)(2,1)}, bf16[768,512]{1,0:T(8,128)(2,1)}, u32[]{:S(2)}, u32[]{:S(2)}) collective-permute-start(bf16[768,512]{1,0:T(8,128)(2,1)} %collective-permute-done.1.refs_1_.refs_4_), channel_id=1, source_target_pairs={{0,4},{4,8},{8,12},{6,2},{10,6},{14,10},{1,5},{5,9},{9,13},{7,3},{... | collective-permute-start | bytes 2359304 | tf_op jit(solution)/shard_map/ppermute | solution.py:255
  77.3 32.4 %collective-permute-done.4.refs_1_.refs_4_ = bf16[768,512]{1,0:T(8,128)(2,1)} collective-permute-done((bf16[768,512]{1,0:T(8,128)(2,1)S(1)}, bf16[768,512]{1,0:T(8,128)(2,1)}, u32[]{:S(2)}, u32[]{:S(2)}) %collective-permute-start.4) | collective-permute-done | bytes 786464 | tf_op jit(solution)/shard_map/ppermute | solution.py:254
  109.7 4.4 %collective-permute-start.5 = (bf16[768,512]{1,0:T(8,128)(2,1)}, bf16[768,512]{1,0:T(8,128)(2,1)}, u32[]{:S(2)}, u32[]{:S(2)}) collective-permute-start(bf16[768,512]{1,0:T(8,128)(2,1)} %collective-permute-done.4.refs_1_.refs_4_), channel_id=1, source_target_pairs={{0,4},{4,8},{8,12},{6,2},{10,6},{14,10},{1,5},{5,9},{9,13},{7,3},{... | collective-permute-start | bytes 2359304 | tf_op jit(solution)/shard_map/ppermute | solution.py:255
  114.1 2.9 reorder_pair.12.refs_0_.refs_3_
  117.0 2.9 reorder_pair.13.refs_0_.refs_3_
  120.1 3.6 collective-permute-start.7
  123.6 5.4 %reorder.1.q_ref = bf16[768,1536]{1,0:T(8,128)(2,1)} custom-call(bf16[768,768]{1,0:T(8,128)(2,1)} %get-tuple-element.72.pick_ref, bf16[768,1536]{1,0:T(8,128)(2,1)} %a_ref.1), custom_call_target="tpu_custom_call" | custom-call | flops 1811939328 | bytes 4718592 | tf_op jit(solution)/shard_map/reorder/pallas_call | solution.py:59
  129.1 2.6 collective-permute-start.9
  131.7 11.9 %attend.7 = (bf16[384,256]{1,0:T(8,128)(2,1)S(1)}, bf16[384,256]{1,0:T(8,128)(2,1)S(1)}) custom-call(bf16[768,1536]{1,0:T(8,128)(2,1)} %reorder.1.q_ref, bf16[768,512]{1,0:T(8,128)(2,1)S(1)} %copy-done.4, bf16[768,512]{1,0:T(8,128)(2,1)} %collective-permute-done.1.refs_1_.refs_4_, bf16[768,512]{1,0:T(8,128)(2,1)} %collective-permute-done.2.refs_2_.refs_5_, ...), custom_call_target="tpu_custom_call" | custom-call | flops 3623878656 | bytes 3145728 | tf_op jit(solution)/shard_map/attend/pallas_call | solution.py:144
  144.3 11.9 %attend.8 = (bf16[384,256]{1,0:T(8,128)(2,1)S(1)}, bf16[384,256]{1,0:T(8,128)(2,1)S(1)}) custom-call(bf16[768,1536]{1,0:T(8,128)(2,1)} %reorder.1.q_ref, bf16[768,512]{1,0:T(8,128)(2,1)S(1)} %copy-done.3, bf16[768,512]{1,0:T(8,128)(2,1)} %collective-permute-done.4.refs_1_.refs_4_, bf16[768,512]{1,0:T(8,128)(2,1)} %collective-permute-done.5.refs_2_.refs_5_, ...), custom_call_target="tpu_custom_call" | custom-call | flops 3623878656 | bytes 3145728 | tf_op jit(solution)/shard_map/attend/pallas_call | solution.py:144
  156.9 0.7 copy-done.19
  157.6 4.4 %collective-permute-done.7.refs_2_.refs_5_ = bf16[768,512]{1,0:T(8,128)(2,1)} collective-permute-done((bf16[768,512]{1,0:T(8,128)(2,1)}, bf16[768,512]{1,0:T(8,128)(2,1)}, u32[]{:S(2)}, u32[]{:S(2)}) %collective-permute-start.7) | collective-permute-done | bytes 786464 | tf_op jit(solution)/shard_map/ppermute | solution.py:255
  162.0 11.9 %attend.9 = (bf16[384,256]{1,0:T(8,128)(2,1)S(1)}, bf16[384,256]{1,0:T(8,128)(2,1)S(1)}) custom-call(bf16[768,1536]{1,0:T(8,128)(2,1)} %reorder.1.q_ref, bf16[768,512]{1,0:T(8,128)(2,1)S(1)} %copy-done.2, bf16[768,512]{1,0:T(8,128)(2,1)} %collective-permute-done.refs_1_.refs_4_, bf16[768,512]{1,0:T(8,128)(2,1)} %collective-permute-done.7.refs_2_.refs_5_, ...), custom_call_target="tpu_custom_call" | custom-call | flops 3623878656 | bytes 3145728 | tf_op jit(solution)/shard_map/attend/pallas_call | solution.py:144
  173.9 4.4 %collective-permute-done.9.refs_2_.refs_5_ = bf16[768,512]{1,0:T(8,128)(2,1)S(1)} collective-permute-done((bf16[768,512]{1,0:T(8,128)(2,1)}, bf16[768,512]{1,0:T(8,128)(2,1)S(1)}, u32[]{:S(2)}, u32[]{:S(2)}) %collective-permute-start.9) | collective-permute-done | bytes 786464 | tf_op jit(solution)/shard_map/ppermute | solution.py:255
  178.3 11.7 %attend.10 = (bf16[384,256]{1,0:T(8,128)(2,1)S(1)}, bf16[384,256]{1,0:T(8,128)(2,1)S(1)}) custom-call(bf16[768,1536]{1,0:T(8,128)(2,1)} %reorder.1.q_ref, bf16[768,512]{1,0:T(8,128)(2,1)S(1)} %copy-done.1, bf16[768,512]{1,0:T(8,128)(2,1)} %collective-permute-done.3.refs_1_.refs_4_, bf16[768,512]{1,0:T(8,128)(2,1)S(1)} %collective-permute-done.9.refs_2_.refs_5_, ...), custom_call_target="tpu_custom_call" | custom-call | flops 3623878656 | bytes 3145728 | tf_op jit(solution)/shard_map/attend/pallas_call | solution.py:144
  190.7 0.7 copy-done.23
  191.4 1.7 collective-permute-start.12
  193.5 4.8 %collective-permute-start.11 = (bf16[768,512]{1,0:T(8,128)(2,1)}, bf16[768,512]{1,0:T(8,128)(2,1)S(1)}, u32[]{:S(2)}, u32[]{:S(2)}) collective-permute-start(bf16[768,512]{1,0:T(8,128)(2,1)} %collective-permute-done.6.refs_1_.refs_4_), channel_id=1, source_target_pairs={{0,4},{4,8},{8,12},{6,2},{10,6},{14,10},{1,5},{5,9},{9,13},{7,3},{... | collective-permute-start | bytes 2359304 | tf_op jit(solution)/shard_map/ppermute | solution.py:255
  198.9 9.2 %collective-permute-done.10.refs_1_.refs_4_ = bf16[768,256]{1,0:T(8,128)(2,1)S(1)} collective-permute-done((bf16[768,256]{1,0:T(8,128)(2,1)S(1)}, bf16[768,256]{1,0:T(8,128)(2,1)S(1)}, u32[]{:S(2)}, u32[]{:S(2)}) %collective-permute-start.10) | collective-permute-done | bytes 393248 | tf_op jit(solution)/shard_map/ppermute | solution.py:254
  208.1 6.2 %collective-permute-done.11.refs_2_.refs_5_ = bf16[768,512]{1,0:T(8,128)(2,1)S(1)} collective-permute-done((bf16[768,512]{1,0:T(8,128)(2,1)}, bf16[768,512]{1,0:T(8,128)(2,1)S(1)}, u32[]{:S(2)}, u32[]{:S(2)}) %collective-permute-start.11) | collective-permute-done | bytes 786464 | tf_op jit(solution)/shard_map/ppermute | solution.py:255
  214.3 11.7 %attend.11 = (bf16[384,256]{1,0:T(8,128)(2,1)S(1)}, bf16[384,256]{1,0:T(8,128)(2,1)S(1)}) custom-call(bf16[768,1536]{1,0:T(8,128)(2,1)} %reorder.1.q_ref, bf16[768,512]{1,0:T(8,128)(2,1)S(1)} %copy-done, bf16[768,512]{1,0:T(8,128)(2,1)} %collective-permute-done.6.refs_1_.refs_4_, bf16[768,512]{1,0:T(8,128)(2,1)S(1)} %collective-permute-done.11.refs_2_.refs_5_, ...), custom_call_target="tpu_custom_call" | custom-call | flops 3623878656 | bytes 3145728 | tf_op jit(solution)/shard_map/attend/pallas_call | solution.py:144
  226.1 19.7 %collective-permute-done.12.refs_16_ = bf16[8,384,384]{2,1,0:T(8,128)(2,1)} collective-permute-done((bf16[8,384,384]{2,1,0:T(8,128)(2,1)}, bf16[8,384,384]{2,1,0:T(8,128)(2,1)}, u32[]{:S(2)}, u32[]{:S(2)}) %collective-permute-start.12) | collective-permute-done | bytes 2359328 | tf_op jit(solution)/shard_map/ppermute | solution.py:276
  245.9 49.0 %collective-permute-done.22.refs_17_ = bf16[8,384,384]{2,1,0:T(8,128)(2,1)S(1)} collective-permute-done((bf16[8,384,384]{2,1,0:T(8,128)(2,1)}, bf16[8,384,384]{2,1,0:T(8,128)(2,1)S(1)}, u32[]{:S(2)}, u32[]{:S(2)}) %collective-permute-start.22) | collective-permute-done | bytes 2359328 | tf_op jit(solution)/shard_map/ppermute | solution.py:276
  294.9 4.3 %collective-permute-start.13 = (bf16[768,256]{1,0:T(8,128)(2,1)S(1)}, bf16[768,256]{1,0:T(8,128)(2,1)S(1)}, u32[]{:S(2)}, u32[]{:S(2)}) collective-permute-start(bf16[768,256]{1,0:T(8,128)(2,1)S(1)} %copy-done.9), channel_id=1, source_target_pairs={{0,4},{4,8},{8,12},{6,2},{10,6},{14,10},{1,5},{5,9},{9,13},{7,3},{... | collective-permute-start | bytes 1179656 | tf_op jit(solution)/shard_map/ppermute | solution.py:255
  299.2 9.0 %collective-permute-done.13.refs_2_.refs_5_ = bf16[768,256]{1,0:T(8,128)(2,1)S(1)} collective-permute-done((bf16[768,256]{1,0:T(8,128)(2,1)S(1)}, bf16[768,256]{1,0:T(8,128)(2,1)S(1)}, u32[]{:S(2)}, u32[]{:S(2)}) %collective-permute-start.13) | collective-permute-done | bytes 393248 | tf_op jit(solution)/shard_map/ppermute | solution.py:255
  308.2 4.4 %collective-permute-start.14 = (bf16[768,256]{1,0:T(8,128)(2,1)S(1)}, bf16[768,256]{1,0:T(8,128)(2,1)S(1)}, u32[]{:S(2)}, u32[]{:S(2)}) collective-permute-start(bf16[768,256]{1,0:T(8,128)(2,1)S(1)} %collective-permute-done.10.refs_1_.refs_4_), channel_id=1, source_target_pairs={{0,4},{4,8},{8,12},{6,2},{10,6},{14,10},{1,5},{5,9},{9,13},{7,3},{... | collective-permute-start | bytes 1179656 | tf_op jit(solution)/shard_map/ppermute | solution.py:255
  312.6 8.2 %collective-permute-done.14.refs_2_.refs_5_ = bf16[768,256]{1,0:T(8,128)(2,1)S(1)} collective-permute-done((bf16[768,256]{1,0:T(8,128)(2,1)S(1)}, bf16[768,256]{1,0:T(8,128)(2,1)S(1)}, u32[]{:S(2)}, u32[]{:S(2)}) %collective-permute-start.14) | collective-permute-done | bytes 393248 | tf_op jit(solution)/shard_map/ppermute | solution.py:255
  320.8 1.4 collective-permute-done.19.refs_11_
  322.4 1.3 collective-permute-done.18.refs_10_
  323.8 1.3 collective-permute-done.17.refs_9_
  325.3 1.3 collective-permute-done.16.refs_8_
  326.7 5.5 %attend.12 = (bf16[384,128]{1,0:T(8,128)(2,1)S(1)}, bf16[384,128]{1,0:T(8,128)(2,1)S(1)}) custom-call(bf16[768,1536]{1,0:T(8,128)(2,1)S(1)} %copy-done.16, bf16[768,256]{1,0:T(8,128)(2,1)S(1)} %copy-done.6, bf16[768,256]{1,0:T(8,128)(2,1)S(1)} %copy-done.9, bf16[768,256]{1,0:T(8,128)(2,1)S(1)} %collective-permute-done.13.refs_2_.refs_5_, ...), custom_call_target="tpu_custom_call" | custom-call | flops 1811939328 | bytes 1572864 | tf_op jit(solution)/shard_map/attend/pallas_call | solution.py:144
  332.2 5.4 %attend.13 = (bf16[384,128]{1,0:T(8,128)(2,1)S(1)}, bf16[384,128]{1,0:T(8,128)(2,1)S(1)}) custom-call(bf16[768,1536]{1,0:T(8,128)(2,1)S(1)} %copy-done.16, bf16[768,256]{1,0:T(8,128)(2,1)S(1)} %copy-done.5, bf16[768,256]{1,0:T(8,128)(2,1)S(1)} %collective-permute-done.10.refs_1_.refs_4_, bf16[768,256]{1,0:T(8,128)(2,1)S(1)} %collective-permute-done.14.refs_2_.refs_5_, ...), custom_call_target="tpu_custom_call" | custom-call | flops 1811939328 | bytes 1572864 | tf_op jit(solution)/shard_map/attend/pallas_call | solution.py:144
  338.3 0.8 collective-permute-done.21.refs_13_
  339.5 15.7 %project.1 = bf16[384,3072]{1,0:T(8,128)(2,1)} custom-call(s32[1]{0:T(128)} %bitcast.shift_ref, bf16[384,256]{1,0:T(8,128)(2,1)S(1)} %copy-done.18, bf16[384,256]{1,0:T(8,128)(2,1)S(1)} %copy-done.20, bf16[384,256]{1,0:T(8,128)(2,1)S(1)} %copy-done.22, bf16[384,256]{1,0:T(8,128)(2,1)S(1)} %copy-done.24, bf16[384,256]{1,0:T(8,128)(2,1)S(1)} %get-tuple-element.103.refs_4_, ...), custom_call_target="tpu_custom_call" | custom-call | flops 7247757312 | bytes 18874368 | tf_op jit(solution)/shard_map/project/pallas_call | solution.py:192
  (95 shorter events, 5.8 us)
Async XLA Ops:
  6.5 184.8 %all-gather.5.cloned.1.call-start = ((), (), s32[]{:S(2)}) async-start(), calls=%async_computation | async-start | bytes 2654208 | tf_op jit(solution)/shard_map/all_gather | solution.py:233
  8.5 184.6 %all-gather.7.cloned.1.call-start = ((), (), s32[]{:S(2)}) async-start(), calls=%async_computation.1 | async-start | bytes 2654208 | tf_op jit(solution)/shard_map/all_gather | solution.py:233
  21.0 8.2 %copy-start.3 = (bf16[768,512]{1,0:T(8,128)(2,1)S(1)}, bf16[768,512]{1,0:T(8,128)(2,1)}, u32[]{:S(2)}) copy-start(bf16[768,512]{1,0:T(8,128)(2,1)} %reorder_pair.8.refs_0_.refs_3_) | copy-start | bytes 2359300
  21.0 99.1 %collective-permute-start = (bf16[768,512]{1,0:T(8,128)(2,1)}, bf16[768,512]{1,0:T(8,128)(2,1)}, u32[]{:S(2)}, u32[]{:S(2)}) collective-permute-start(bf16[768,512]{1,0:T(8,128)(2,1)} %reorder_pair.9.refs_0_.refs_3_), channel_id=1, source_target_pairs={{0,2},{2,0},{4,6},{6,4},{8,10},{10,8},{12,14},{14,12},{1,3},{3,1},... | collective-permute-start | bytes 2359304 | tf_op jit(solution)/shard_map/ppermute | solution.py:254
  24.0 48.8 %collective-permute-start.1 = (bf16[768,512]{1,0:T(8,128)(2,1)S(1)}, bf16[768,512]{1,0:T(8,128)(2,1)}, u32[]{:S(2)}, u32[]{:S(2)}) collective-permute-start(bf16[768,512]{1,0:T(8,128)(2,1)S(1)} %copy-done.4), channel_id=1, source_target_pairs={{0,2},{2,0},{4,6},{6,4},{8,10},{10,8},{12,14},{14,12},{1,3},{3,1},... | collective-permute-start | bytes 2359304 | tf_op jit(solution)/shard_map/ppermute | solution.py:254
  27.2 101.8 %collective-permute-start.3 = (bf16[768,512]{1,0:T(8,128)(2,1)}, bf16[768,512]{1,0:T(8,128)(2,1)}, u32[]{:S(2)}, u32[]{:S(2)}) collective-permute-start(bf16[768,512]{1,0:T(8,128)(2,1)} %reorder_pair.10.refs_0_.refs_3_), channel_id=1, source_target_pairs={{0,2},{2,0},{4,6},{6,4},{8,10},{10,8},{12,14},{14,12},{1,3},{3,1},... | collective-permute-start | bytes 2359304 | tf_op jit(solution)/shard_map/ppermute | solution.py:254
  29.2 80.5 %collective-permute-start.4 = (bf16[768,512]{1,0:T(8,128)(2,1)S(1)}, bf16[768,512]{1,0:T(8,128)(2,1)}, u32[]{:S(2)}, u32[]{:S(2)}) collective-permute-start(bf16[768,512]{1,0:T(8,128)(2,1)S(1)} %copy-done.3), channel_id=1, source_target_pairs={{0,2},{2,0},{4,6},{6,4},{8,10},{10,8},{12,14},{14,12},{1,3},{3,1},... | collective-permute-start | bytes 2359304 | tf_op jit(solution)/shard_map/ppermute | solution.py:254
  32.4 125.2 %collective-permute-start.6 = (bf16[768,512]{1,0:T(8,128)(2,1)}, bf16[768,512]{1,0:T(8,128)(2,1)}, u32[]{:S(2)}, u32[]{:S(2)}) collective-permute-start(bf16[768,512]{1,0:T(8,128)(2,1)} %reorder_pair.11.refs_0_.refs_3_), channel_id=1, source_target_pairs={{0,2},{2,0},{4,6},{6,4},{8,10},{10,8},{12,14},{14,12},{1,3},{3,1},... | collective-permute-start | bytes 2359304 | tf_op jit(solution)/shard_map/ppermute | solution.py:254
  72.9 56.3 %collective-permute-start.2 = (bf16[768,512]{1,0:T(8,128)(2,1)}, bf16[768,512]{1,0:T(8,128)(2,1)}, u32[]{:S(2)}, u32[]{:S(2)}) collective-permute-start(bf16[768,512]{1,0:T(8,128)(2,1)} %collective-permute-done.1.refs_1_.refs_4_), channel_id=1, source_target_pairs={{0,4},{4,8},{8,12},{6,2},{10,6},{14,10},{1,5},{5,9},{9,13},{7,3},{... | collective-permute-start | bytes 2359304 | tf_op jit(solution)/shard_map/ppermute | solution.py:255
  109.7 34.5 %collective-permute-start.5 = (bf16[768,512]{1,0:T(8,128)(2,1)}, bf16[768,512]{1,0:T(8,128)(2,1)}, u32[]{:S(2)}, u32[]{:S(2)}) collective-permute-start(bf16[768,512]{1,0:T(8,128)(2,1)} %collective-permute-done.4.refs_1_.refs_4_), channel_id=1, source_target_pairs={{0,4},{4,8},{8,12},{6,2},{10,6},{14,10},{1,5},{5,9},{9,13},{7,3},{... | collective-permute-start | bytes 2359304 | tf_op jit(solution)/shard_map/ppermute | solution.py:255
  120.0 9.0 %copy-start.6 = (bf16[768,256]{1,0:T(8,128)(2,1)S(1)}, bf16[768,256]{1,0:T(8,128)(2,1)}, u32[]{:S(2)}) copy-start(bf16[768,256]{1,0:T(8,128)(2,1)} %reorder_pair.12.refs_0_.refs_3_) | copy-start | bytes 1179652
  120.1 41.9 %collective-permute-start.7 = (bf16[768,512]{1,0:T(8,128)(2,1)}, bf16[768,512]{1,0:T(8,128)(2,1)}, u32[]{:S(2)}, u32[]{:S(2)}) collective-permute-start(bf16[768,512]{1,0:T(8,128)(2,1)} %collective-permute-done.refs_1_.refs_4_), channel_id=1, source_target_pairs={{0,4},{4,8},{8,12},{6,2},{10,6},{14,10},{1,5},{5,9},{9,13},{7,3},{... | collective-permute-start | bytes 2359304 | tf_op jit(solution)/shard_map/ppermute | solution.py:255
  129.0 44.9 %collective-permute-start.8 = (bf16[768,256]{1,0:T(8,128)(2,1)S(1)}, bf16[768,256]{1,0:T(8,128)(2,1)S(1)}, u32[]{:S(2)}, u32[]{:S(2)}) collective-permute-start(bf16[768,256]{1,0:T(8,128)(2,1)S(1)} %copy-done.6), channel_id=1, source_target_pairs={{0,2},{2,0},{4,6},{6,4},{8,10},{10,8},{12,14},{14,12},{1,3},{3,1},... | collective-permute-start | bytes 1179656 | tf_op jit(solution)/shard_map/ppermute | solution.py:254
  129.1 49.1 %collective-permute-start.9 = (bf16[768,512]{1,0:T(8,128)(2,1)}, bf16[768,512]{1,0:T(8,128)(2,1)S(1)}, u32[]{:S(2)}, u32[]{:S(2)}) collective-permute-start(bf16[768,512]{1,0:T(8,128)(2,1)} %collective-permute-done.3.refs_1_.refs_4_), channel_id=1, source_target_pairs={{0,4},{4,8},{8,12},{6,2},{10,6},{14,10},{1,5},{5,9},{9,13},{7,3},{... | collective-permute-start | bytes 2359304 | tf_op jit(solution)/shard_map/ppermute | solution.py:255
  144.3 17.7 %copy-start.2 = (bf16[768,512]{1,0:T(8,128)(2,1)S(1)}, bf16[768,512]{1,0:T(8,128)(2,1)}, u32[]{:S(2)}) copy-start(bf16[768,512]{1,0:T(8,128)(2,1)} %reorder_pair.9.refs_0_.refs_3_) | copy-start | bytes 2359300
  157.6 20.7 %copy-start.1 = (bf16[768,512]{1,0:T(8,128)(2,1)S(1)}, bf16[768,512]{1,0:T(8,128)(2,1)}, u32[]{:S(2)}) copy-start(bf16[768,512]{1,0:T(8,128)(2,1)} %reorder_pair.10.refs_0_.refs_3_) | copy-start | bytes 2359300
  173.9 16.1 %copy-start.12 = (bf16[384,256]{1,0:T(8,128)(2,1)}, bf16[384,256]{1,0:T(8,128)(2,1)S(1)}, u32[]{:S(2)}) copy-start(bf16[384,256]{1,0:T(8,128)(2,1)S(1)} %get-tuple-element.120) | copy-start | bytes 589828
  173.9 16.1 %copy-start.21 = (bf16[384,256]{1,0:T(8,128)(2,1)}, bf16[384,256]{1,0:T(8,128)(2,1)S(1)}, u32[]{:S(2)}) copy-start(bf16[384,256]{1,0:T(8,128)(2,1)S(1)} %get-tuple-element.90.refs_2_) | copy-start | bytes 589828
  173.9 24.4 %copy-start.5 = (bf16[768,256]{1,0:T(8,128)(2,1)S(1)}, bf16[768,256]{1,0:T(8,128)(2,1)}, u32[]{:S(2)}) copy-start(bf16[768,256]{1,0:T(8,128)(2,1)} %reorder_pair.13.refs_0_.refs_3_) | copy-start | bytes 1179652
  173.9 40.4 %copy-start = (bf16[768,512]{1,0:T(8,128)(2,1)S(1)}, bf16[768,512]{1,0:T(8,128)(2,1)}, u32[]{:S(2)}) copy-start(bf16[768,512]{1,0:T(8,128)(2,1)} %reorder_pair.11.refs_0_.refs_3_) | copy-start | bytes 2359300
  173.9 16.1 %copy-start.8 = (bf16[768,256]{1,0:T(8,128)(2,1)}, bf16[768,256]{1,0:T(8,128)(2,1)S(1)}, u32[]{:S(2)}) copy-start(bf16[768,256]{1,0:T(8,128)(2,1)S(1)} %collective-permute-done.8.refs_1_.refs_4_) | copy-start | bytes 1179652
  191.4 54.5 %collective-permute-start.12 = (bf16[8,384,384]{2,1,0:T(8,128)(2,1)}, bf16[8,384,384]{2,1,0:T(8,128)(2,1)}, u32[]{:S(2)}, u32[]{:S(2)}) collective-permute-start(bf16[8,384,384]{2,1,0:T(8,128)(2,1)} %bitcast.18), channel_id=1, source_target_pairs={{0,16},{16,0},{1,17},{17,1},{2,18},{18,2},{3,19},{19,3},{4,20},{20... | collective-permute-start | bytes 7077896 | tf_op jit(solution)/shard_map/ppermute | solution.py:276
  193.1 32.9 %copy-start.7 = (bf16[3072,384]{1,0:T(8,128)(2,1)S(1)}, bf16[3072,384]{1,0:T(8,128)(2,1)}, u32[]{:S(2)}) copy-start(bf16[3072,384]{1,0:T(8,128)(2,1)} %all-gather.5.cloned.1.call-done) | copy-start | bytes 7077892
  193.1 101.8 %copy-start.9 = (bf16[768,256]{1,0:T(8,128)(2,1)S(1)}, bf16[768,256]{1,0:T(8,128)(2,1)}, u32[]{:S(2)}) copy-start(bf16[768,256]{1,0:T(8,128)(2,1)} %copy-done.8) | copy-start | bytes 1179652
  193.1 129.1 %copy-start.15 = (bf16[384,256]{1,0:T(8,128)(2,1)S(1)}, bf16[384,256]{1,0:T(8,128)(2,1)}, u32[]{:S(2)}) copy-start(bf16[384,256]{1,0:T(8,128)(2,1)} %copy-done.14) | copy-start | bytes 589828
  193.1 130.6 %copy-start.13 = (bf16[384,256]{1,0:T(8,128)(2,1)S(1)}, bf16[384,256]{1,0:T(8,128)(2,1)}, u32[]{:S(2)}) copy-start(bf16[384,256]{1,0:T(8,128)(2,1)} %copy-done.12) | copy-start | bytes 589828
  193.1 132.0 %copy-start.11 = (bf16[384,256]{1,0:T(8,128)(2,1)S(1)}, bf16[384,256]{1,0:T(8,128)(2,1)}, u32[]{:S(2)}) copy-start(bf16[384,256]{1,0:T(8,128)(2,1)} %copy-done.10) | copy-start | bytes 589828
  193.1 133.6 %copy-start.16 = (bf16[768,1536]{1,0:T(8,128)(2,1)S(1)}, bf16[768,1536]{1,0:T(8,128)(2,1)}, u32[]{:S(2)}) copy-start(bf16[768,1536]{1,0:T(8,128)(2,1)} %reorder.1.q_ref) | copy-start | bytes 7077892
  193.1 101.7 %collective-permute-start.22 = (bf16[8,384,384]{2,1,0:T(8,128)(2,1)}, bf16[8,384,384]{2,1,0:T(8,128)(2,1)S(1)}, u32[]{:S(2)}, u32[]{:S(2)}) collective-permute-start(bf16[8,384,384]{2,1,0:T(8,128)(2,1)} %bitcast.22), channel_id=1, source_target_pairs={{0,16},{16,0},{1,17},{17,1},{2,18},{18,2},{3,19},{19,3},{4,20},{20... | collective-permute-start | bytes 7077896 | tf_op jit(solution)/shard_map/ppermute | solution.py:276
  193.5 20.8 %collective-permute-start.11 = (bf16[768,512]{1,0:T(8,128)(2,1)}, bf16[768,512]{1,0:T(8,128)(2,1)S(1)}, u32[]{:S(2)}, u32[]{:S(2)}) collective-permute-start(bf16[768,512]{1,0:T(8,128)(2,1)} %collective-permute-done.6.refs_1_.refs_4_), channel_id=1, source_target_pairs={{0,4},{4,8},{8,12},{6,2},{10,6},{14,10},{1,5},{5,9},{9,13},{7,3},{... | collective-permute-start | bytes 2359304 | tf_op jit(solution)/shard_map/ppermute | solution.py:255
  198.3 9.8 %collective-permute-start.10 = (bf16[768,256]{1,0:T(8,128)(2,1)S(1)}, bf16[768,256]{1,0:T(8,128)(2,1)S(1)}, u32[]{:S(2)}, u32[]{:S(2)}) collective-permute-start(bf16[768,256]{1,0:T(8,128)(2,1)S(1)} %copy-done.5), channel_id=1, source_target_pairs={{0,2},{2,0},{4,6},{6,4},{8,10},{10,8},{12,14},{14,12},{1,3},{3,1},... | collective-permute-start | bytes 1179656 | tf_op jit(solution)/shard_map/ppermute | solution.py:254
  208.1 130.0 %collective-permute-start.24 = (bf16[8,384,384]{2,1,0:T(8,128)(2,1)}, bf16[8,384,384]{2,1,0:T(8,128)(2,1)}, u32[]{:S(2)}, u32[]{:S(2)}) collective-permute-start(bf16[8,384,384]{2,1,0:T(8,128)(2,1)} %bitcast.23), channel_id=1, source_target_pairs={{0,1},{1,0},{2,3},{3,2},{4,5},{5,4},{6,7},{7,6},{8,9},{9,8},{10,11... | collective-permute-start | bytes 7077896 | tf_op jit(solution)/shard_map/ppermute | solution.py:280
  226.0 112.2 %collective-permute-start.23 = (bf16[8,384,384]{2,1,0:T(8,128)(2,1)S(1)}, bf16[8,384,384]{2,1,0:T(8,128)(2,1)}, u32[]{:S(2)}, u32[]{:S(2)}) collective-permute-start(bf16[8,384,384]{2,1,0:T(8,128)(2,1)S(1)} %bitcast.19), channel_id=1, source_target_pairs={{0,1},{1,0},{2,3},{3,2},{4,5},{5,4},{6,7},{7,6},{8,9},{9,8},{10,11... | collective-permute-start | bytes 7077896 | tf_op jit(solution)/shard_map/ppermute | solution.py:280
  245.9 93.6 %collective-permute-start.25 = (bf16[8,384,384]{2,1,0:T(8,128)(2,1)}, bf16[8,384,384]{2,1,0:T(8,128)(2,1)}, u32[]{:S(2)}, u32[]{:S(2)}) collective-permute-start(bf16[8,384,384]{2,1,0:T(8,128)(2,1)} %collective-permute-done.12.refs_16_), channel_id=1, source_target_pairs={{0,1},{1,0},{2,3},{3,2},{4,5},{5,4},{6,7},{7,6},{8,9},{9,8},{10,11... | collective-permute-start | bytes 7077896 | tf_op jit(solution)/shard_map/ppermute | solution.py:280
  294.9 37.3 %copy-start.26 = (bf16[8,384,384]{2,1,0:T(8,128)(2,1)}, bf16[8,384,384]{2,1,0:T(8,128)(2,1)S(1)}, u32[]{:S(2)}) copy-start(bf16[8,384,384]{2,1,0:T(8,128)(2,1)S(1)} %collective-permute-done.22.refs_17_) | copy-start | bytes 7077892
  294.9 44.6 %collective-permute-start.26 = (bf16[8,384,384]{2,1,0:T(8,128)(2,1)S(1)}, bf16[8,384,384]{2,1,0:T(8,128)(2,1)}, u32[]{:S(2)}, u32[]{:S(2)}) collective-permute-start(bf16[8,384,384]{2,1,0:T(8,128)(2,1)S(1)} %collective-permute-done.22.refs_17_), channel_id=1, source_target_pairs={{0,1},{1,0},{2,3},{3,2},{4,5},{5,4},{6,7},{7,6},{8,9},{9,8},{10,11... | collective-permute-start | bytes 7077896 | tf_op jit(solution)/shard_map/ppermute | solution.py:280
  294.9 13.3 %collective-permute-start.13 = (bf16[768,256]{1,0:T(8,128)(2,1)S(1)}, bf16[768,256]{1,0:T(8,128)(2,1)S(1)}, u32[]{:S(2)}, u32[]{:S(2)}) collective-permute-start(bf16[768,256]{1,0:T(8,128)(2,1)S(1)} %copy-done.9), channel_id=1, source_target_pairs={{0,4},{4,8},{8,12},{6,2},{10,6},{14,10},{1,5},{5,9},{9,13},{7,3},{... | collective-permute-start | bytes 1179656 | tf_op jit(solution)/shard_map/ppermute | solution.py:255
  308.2 12.6 %collective-permute-start.14 = (bf16[768,256]{1,0:T(8,128)(2,1)S(1)}, bf16[768,256]{1,0:T(8,128)(2,1)S(1)}, u32[]{:S(2)}, u32[]{:S(2)}) collective-permute-start(bf16[768,256]{1,0:T(8,128)(2,1)S(1)} %collective-permute-done.10.refs_1_.refs_4_), channel_id=1, source_target_pairs={{0,4},{4,8},{8,12},{6,2},{10,6},{14,10},{1,5},{5,9},{9,13},{7,3},{... | collective-permute-start | bytes 1179656 | tf_op jit(solution)/shard_map/ppermute | solution.py:255
  320.8 1.4 collective-permute-start.19
  322.2 1.4 collective-permute-start.18
  323.7 1.4 collective-permute-start.17
  325.1 1.4 collective-permute-start.16
  326.6 11.1 %collective-permute-start.15 = (bf16[384,256]{1,0:T(8,128)(2,1)S(1)}, bf16[384,256]{1,0:T(8,128)(2,1)S(1)}, u32[]{:S(2)}, u32[]{:S(2)}) collective-permute-start(bf16[384,256]{1,0:T(8,128)(2,1)S(1)} %get-tuple-element.118), channel_id=1, source_target_pairs={{0,1},{1,0},{2,3},{3,2},{4,5},{5,4},{6,7},{7,6},{8,9},{9,8},{10,11... | collective-permute-start | bytes 589832 | tf_op jit(solution)/shard_map/ppermute | solution.py:278
  332.2 7.3 %copy-start.18 = (bf16[384,256]{1,0:T(8,128)(2,1)S(1)}, bf16[384,256]{1,0:T(8,128)(2,1)}, u32[]{:S(2)}) copy-start(bf16[384,256]{1,0:T(8,128)(2,1)} %copy-done.17) | copy-start | bytes 589828
  332.2 7.2 %copy-start.20 = (bf16[384,256]{1,0:T(8,128)(2,1)S(1)}, bf16[384,256]{1,0:T(8,128)(2,1)}, u32[]{:S(2)}) copy-start(bf16[384,256]{1,0:T(8,128)(2,1)} %copy-done.19) | copy-start | bytes 589828
  332.2 7.2 %copy-start.22 = (bf16[384,256]{1,0:T(8,128)(2,1)S(1)}, bf16[384,256]{1,0:T(8,128)(2,1)}, u32[]{:S(2)}) copy-start(bf16[384,256]{1,0:T(8,128)(2,1)} %copy-done.21) | copy-start | bytes 589828
  337.7 1.4 collective-permute-start.21
  338.1 1.3 collective-permute-start.20
  (8 other events, 24.2 us)
Sparse Core Ops, SparseCore 0:
  9.5 67.6 all-gather.4
  79.4 70.5 all-gather.6

commit v3 on v2

--- a/solution.py
+++ b/solution.py
@@ -11,7 +11,7 @@
 HD = 128
 GW = 3
 PIECES = 2
-TIES = (1, 3)
+TIES = (0, 2)
 HIDDEN = -1e30
 
 
@@ -99,8 +99,7 @@
     factor = HD ** (-0.5) * math.log2(math.e)
     dims = (((1,), (1,)), ((), ()))
 
-    @pl.loop(0, rows // tile_tok)
-    def _(tile):
+    def one_tile(tile):
         place = pl.ds(pl.multiple_of(tile * tile_tok, tile_tok), tile_tok)
         part_q = q_ref[place, :]
         scores = [
@@ -120,6 +119,11 @@
                 expon.astype(jnp.bfloat16), v_ref[...], preferred_element_type=jnp.float32
             )
         att_ref[place, :] = (total / denom).astype(jnp.bfloat16)
+
+    @pl.loop(0, rows // (2 * tile_tok))
+    def _(index):
+        one_tile(2 * index)
+        one_tile(2 * index + 1)
 
     att = att_ref[...]
     own_ref[...] = jnp.dot(
@@ -259,7 +263,13 @@
     for chunk in chunks:
         ahead = min(chunk + 2, len(sizes) - 1)
         queries, near[ahead] = lax.optimization_barrier((queries, near[ahead]))
-        if chunk == TIES[1] + 2:
+        after = min(chunk + 1, len(sizes) - 1)
+        queries, far[after] = lax.optimization_barrier((queries, far[after]))
+        if chunk in TIES:
+            piece = TIES.index(chunk)
+            queries, gathered[piece] = lax.optimization_barrier((queries, gathered[piece]))
+            crossed.append(lax.ppermute(gathered[piece], "clips", paired))
+        if chunk == len(sizes) - 2:
             queries, crossed[0] = lax.optimization_barrier((queries, crossed[0]))
         kept, sent = attend(
             queries,
@@ -270,10 +280,6 @@
             tile_tok,
         )
         queries, kept = lax.optimization_barrier((queries, kept))
-        if chunk in TIES:
-            piece = TIES.index(chunk)
-            gathered[piece], kept = lax.optimization_barrier((gathered[piece], kept))
-            crossed.append(lax.ppermute(gathered[piece], "clips", paired))
         own.append(kept)
         other.append(lax.ppermute(sent, "head", across))
     weights = gathered + crossed

time: 364 us -> 318 us (0.87)
  waiting for transfers between devices: 188 us -> 148 us
  Pallas kernels: 113 us -> 104 us
    ppermute x2, waiting for transfers between devices: 68.7 us -> 42.7 us  [on_device(): crossed.append(lax.ppermute(gathered[piece], 'clips', paired))]
    ppermute x7, waiting for transfers between devices: 79.5 us -> 67.7 us  [on_device(): near = [lax.ppermute(pair, 'tm', beside) for pair in mine]]
    pallas_call x7, Pallas kernels: 70 us -> 60.7 us  [attend(): pl.pallas_call(functools.partial(attend_kernel, tile_tok), grid=(heads,),...]
    ppermute x7, waiting for transfers between devices: 32.2 us -> 28.4 us  [on_device(): far = [lax.ppermute(pair, 'tm', onward) for pair in near]]
  transfers between devices with their start and end apart: 29 -> 29, of which waited for: 16 -> 15; matrix products, arithmetic and copies ran while one was open for 1% -> 1% of each run, Pallas kernels for 27% -> 28%
where the time goes in v3:
time: 318 us; the launch traced here: 317 us
  waiting for transfers between devices  148 us (47%)
  Pallas kernels  104 us (33%)
  starting transfers between devices  42.4 us (13%)
  between operations  13.8 us (4%)
  local copies, waits for them, and re-layouts  6.56 us (2%)
    ppermute x7, waiting for transfers between devices, on_device(): near = [lax.ppermute(pair, 'tm', beside) for pair in mine]  67.7 us
    pallas_call x7, Pallas kernels, attend(): pl.pallas_call(functools.partial(attend_kernel, tile_tok), grid=(heads,),...  60.7 us
    ppermute x2, waiting for transfers between devices, on_device(): crossed.append(lax.ppermute(gathered[piece], 'clips', paired))  42.7 us
    ppermute x7, waiting for transfers between devices, on_device(): far = [lax.ppermute(pair, 'tm', onward) for pair in near]  28.4 us
    ppermute x7, starting transfers between devices, on_device(): far = [lax.ppermute(pair, 'tm', onward) for pair in near]  28 us
    pallas_call x7, Pallas kernels, reorder_pair(): pl.pallas_call(reorder_pair_kernel, grid=(1,), in_specs=[pl.BlockSpec((ro...  21.8 us
    pallas_call x1, Pallas kernels, project(): pl.pallas_call(functools.partial(project_kernel, count, starts), grid=(bl...  15.9 us
    ppermute x7, starting transfers between devices, on_device(): near = [lax.ppermute(pair, 'tm', beside) for pair in mine]  9.17 us
  transfers between devices with their start and end apart: 29, of which 15 were waited for; matrix products, arithmetic and copies ran while one was open for 1% of the time, Pallas kernels for 28%

profile of v3, /device:TPU:0, one launch (start us, length us, event | category | flops | bytes accessed | tf_op | source)
XLA Modules:
  0.0 316.9 jit_solution(2313041594988593139)
XLA Ops:
  6.5 1.9 constant_dynamic-slice_fusion
  8.5 0.7 all-gather.7.cloned.1.call-update
  9.3 0.7 reduce
  10.0 1.5 compare_convert_fusion
  11.4 3.1 reorder_pair.7.refs_0_.refs_3_
  14.6 3.1 reorder_pair.8.refs_0_.refs_3_
  17.7 3.4 %reorder_pair.9.refs_0_.refs_3_ = bf16[768,512]{1,0:T(8,128)(2,1)} custom-call(bf16[768,768]{1,0:T(8,128)(2,1)} %get-tuple-element.86.pick_ref, bf16[768,1536]{1,0:T(8,128)(2,1)} %k_ref.13, bf16[768,1536]{1,0:T(8,128)(2,1)} %v_ref.13), custom_call_target="tpu_custom_call" | custom-call | flops 603979776 | bytes 1572864 | tf_op jit(solution)/shard_map/reorder_pair/pallas_call | solution.py:77
  21.1 3.0 collective-permute-start
  24.2 2.0 collective-permute-start.3
  26.2 3.1 reorder_pair.10.refs_0_.refs_3_
  29.4 3.2 %reorder_pair.11.refs_0_.refs_3_ = bf16[768,512]{1,0:T(8,128)(2,1)} custom-call(bf16[768,768]{1,0:T(8,128)(2,1)} %get-tuple-element.86.pick_ref, bf16[768,1536]{1,0:T(8,128)(2,1)} %k_ref.13, bf16[768,1536]{1,0:T(8,128)(2,1)} %v_ref.13), custom_call_target="tpu_custom_call" | custom-call | flops 603979776 | bytes 1572864 | tf_op jit(solution)/shard_map/reorder_pair/pallas_call | solution.py:77
  32.6 2.0 collective-permute-start.7
  35.2 37.6 %collective-permute-done.1.refs_1_.refs_4_ = bf16[768,512]{1,0:T(8,128)(2,1)} collective-permute-done((bf16[768,512]{1,0:T(8,128)(2,1)S(1)}, bf16[768,512]{1,0:T(8,128)(2,1)}, u32[]{:S(2)}, u32[]{:S(2)}) %collective-permute-start.1) | collective-permute-done | bytes 786464 | tf_op jit(solution)/shard_map/ppermute | solution.py:258
  72.9 4.4 %collective-permute-start.2 = (bf16[768,512]{1,0:T(8,128)(2,1)}, bf16[768,512]{1,0:T(8,128)(2,1)}, u32[]{:S(2)}, u32[]{:S(2)}) collective-permute-start(bf16[768,512]{1,0:T(8,128)(2,1)} %collective-permute-done.1.refs_1_.refs_4_), channel_id=1, source_target_pairs={{0,4},{4,8},{8,12},{6,2},{10,6},{14,10},{1,5},{5,9},{9,13},{7,3},{... | collective-permute-start | bytes 2359304 | tf_op jit(solution)/shard_map/ppermute | solution.py:259
  77.3 13.3 %collective-permute-done.3.refs_1_.refs_4_ = bf16[768,512]{1,0:T(8,128)(2,1)} collective-permute-done((bf16[768,512]{1,0:T(8,128)(2,1)S(1)}, bf16[768,512]{1,0:T(8,128)(2,1)}, u32[]{:S(2)}, u32[]{:S(2)}) %collective-permute-start.3) | collective-permute-done | bytes 786464 | tf_op jit(solution)/shard_map/ppermute | solution.py:258
  90.5 4.5 %collective-permute-start.4 = (bf16[768,512]{1,0:T(8,128)(2,1)}, bf16[768,512]{1,0:T(8,128)(2,1)}, u32[]{:S(2)}, u32[]{:S(2)}) collective-permute-start(bf16[768,512]{1,0:T(8,128)(2,1)} %collective-permute-done.3.refs_1_.refs_4_), channel_id=1, source_target_pairs={{0,4},{4,8},{8,12},{6,2},{10,6},{14,10},{1,5},{5,9},{9,13},{7,3},{... | collective-permute-start | bytes 2359304 | tf_op jit(solution)/shard_map/ppermute | solution.py:259
  95.1 3.4 %collective-permute-start.6 = (bf16[768,512]{1,0:T(8,128)(2,1)}, bf16[768,512]{1,0:T(8,128)(2,1)}, u32[]{:S(2)}, u32[]{:S(2)}) collective-permute-start(bf16[768,512]{1,0:T(8,128)(2,1)} %collective-permute-done.refs_1_.refs_4_), channel_id=1, source_target_pairs={{0,4},{4,8},{8,12},{6,2},{10,6},{14,10},{1,5},{5,9},{9,13},{7,3},{... | collective-permute-start | bytes 2359304 | tf_op jit(solution)/shard_map/ppermute | solution.py:259
  98.5 2.9 reorder_pair.12.refs_0_.refs_3_
  101.4 2.9 reorder_pair.13.refs_0_.refs_3_
  104.5 5.2 %collective-permute-done.5.refs_1_.refs_4_ = bf16[768,512]{1,0:T(8,128)(2,1)} collective-permute-done((bf16[768,512]{1,0:T(8,128)(2,1)}, bf16[768,512]{1,0:T(8,128)(2,1)}, u32[]{:S(2)}, u32[]{:S(2)}) %collective-permute-start.5) | collective-permute-done | bytes 786464 | tf_op jit(solution)/shard_map/ppermute | solution.py:258
  109.7 4.4 %collective-permute-start.8 = (bf16[768,512]{1,0:T(8,128)(2,1)}, bf16[768,512]{1,0:T(8,128)(2,1)}, u32[]{:S(2)}, u32[]{:S(2)}) collective-permute-start(bf16[768,512]{1,0:T(8,128)(2,1)} %collective-permute-done.5.refs_1_.refs_4_), channel_id=1, source_target_pairs={{0,4},{4,8},{8,12},{6,2},{10,6},{14,10},{1,5},{5,9},{9,13},{7,3},{... | collective-permute-start | bytes 2359304 | tf_op jit(solution)/shard_map/ppermute | solution.py:259
  114.2 5.4 %reorder.1.q_ref = bf16[768,1536]{1,0:T(8,128)(2,1)} custom-call(bf16[768,768]{1,0:T(8,128)(2,1)} %get-tuple-element.86.pick_ref, bf16[768,1536]{1,0:T(8,128)(2,1)} %a_ref.1), custom_call_target="tpu_custom_call" | custom-call | flops 1811939328 | bytes 4718592 | tf_op jit(solution)/shard_map/reorder/pallas_call | solution.py:59
  119.5 9.6 %collective-permute-done.4.refs_2_.refs_5_ = bf16[768,512]{1,0:T(8,128)(2,1)} collective-permute-done((bf16[768,512]{1,0:T(8,128)(2,1)}, bf16[768,512]{1,0:T(8,128)(2,1)}, u32[]{:S(2)}, u32[]{:S(2)}) %collective-permute-start.4) | collective-permute-done | bytes 786464 | tf_op jit(solution)/shard_map/ppermute | solution.py:259
  129.2 10.2 %attend.7 = (bf16[384,256]{1,0:T(8,128)(2,1)S(1)}, bf16[384,256]{1,0:T(8,128)(2,1)S(1)}) custom-call(bf16[768,1536]{1,0:T(8,128)(2,1)} %reorder.1.q_ref, bf16[768,512]{1,0:T(8,128)(2,1)S(1)} %copy-done.4, bf16[768,512]{1,0:T(8,128)(2,1)} %collective-permute-done.3.refs_1_.refs_4_, bf16[768,512]{1,0:T(8,128)(2,1)} %collective-permute-done.4.refs_2_.refs_5_, ...), custom_call_target="tpu_custom_call" | custom-call | flops 3623878656 | bytes 3145728 | tf_op jit(solution)/shard_map/attend/pallas_call | solution.py:148
  140.7 16.1 %collective-permute-done.6.refs_2_.refs_5_ = bf16[768,512]{1,0:T(8,128)(2,1)} collective-permute-done((bf16[768,512]{1,0:T(8,128)(2,1)}, bf16[768,512]{1,0:T(8,128)(2,1)}, u32[]{:S(2)}, u32[]{:S(2)}) %collective-permute-start.6) | collective-permute-done | bytes 786464 | tf_op jit(solution)/shard_map/ppermute | solution.py:259
  156.8 0.9 copy-done.8
  157.7 10.2 %attend.8 = (bf16[384,256]{1,0:T(8,128)(2,1)S(1)}, bf16[384,256]{1,0:T(8,128)(2,1)S(1)}) custom-call(bf16[768,1536]{1,0:T(8,128)(2,1)} %reorder.1.q_ref, bf16[768,512]{1,0:T(8,128)(2,1)S(1)} %copy-done.3, bf16[768,512]{1,0:T(8,128)(2,1)} %collective-permute-done.1.refs_1_.refs_4_, bf16[768,512]{1,0:T(8,128)(2,1)} %collective-permute-done.2.refs_2_.refs_5_, ...), custom_call_target="tpu_custom_call" | custom-call | flops 3623878656 | bytes 3145728 | tf_op jit(solution)/shard_map/attend/pallas_call | solution.py:148
  169.3 2.6 collective-permute-done.8.refs_2_.refs_5_
  171.9 1.5 collective-permute-start.14
  173.9 4.4 %collective-permute-start.10 = (bf16[768,512]{1,0:T(8,128)(2,1)}, bf16[768,512]{1,0:T(8,128)(2,1)S(1)}, u32[]{:S(2)}, u32[]{:S(2)}) collective-permute-start(bf16[768,512]{1,0:T(8,128)(2,1)} %collective-permute-done.7.refs_1_.refs_4_), channel_id=1, source_target_pairs={{0,4},{4,8},{8,12},{6,2},{10,6},{14,10},{1,5},{5,9},{9,13},{7,3},{... | collective-permute-start | bytes 2359304 | tf_op jit(solution)/shard_map/ppermute | solution.py:259
  178.5 2.0 collective-permute-start.11
  180.5 10.0 %collective-permute-done.9.refs_1_.refs_4_ = bf16[768,256]{1,0:T(8,128)(2,1)S(1)} collective-permute-done((bf16[768,256]{1,0:T(8,128)(2,1)S(1)}, bf16[768,256]{1,0:T(8,128)(2,1)S(1)}, u32[]{:S(2)}, u32[]{:S(2)}) %collective-permute-start.9) | collective-permute-done | bytes 393248 | tf_op jit(solution)/shard_map/ppermute | solution.py:258
  190.5 3.3 %collective-permute-start.12 = (bf16[768,256]{1,0:T(8,128)(2,1)S(1)}, bf16[768,256]{1,0:T(8,128)(2,1)S(1)}, u32[]{:S(2)}, u32[]{:S(2)}) collective-permute-start(bf16[768,256]{1,0:T(8,128)(2,1)S(1)} %collective-permute-done.9.refs_1_.refs_4_), channel_id=1, source_target_pairs={{0,4},{4,8},{8,12},{6,2},{10,6},{14,10},{1,5},{5,9},{9,13},{7,3},{... | collective-permute-start | bytes 1179656 | tf_op jit(solution)/shard_map/ppermute | solution.py:259
  193.8 1.5 collective-permute-done.11.refs_1_.refs_4_
  195.4 3.5 %collective-permute-start.13 = (bf16[768,256]{1,0:T(8,128)(2,1)S(1)}, bf16[768,256]{1,0:T(8,128)(2,1)S(1)}, u32[]{:S(2)}, u32[]{:S(2)}) collective-permute-start(bf16[768,256]{1,0:T(8,128)(2,1)S(1)} %collective-permute-done.11.refs_1_.refs_4_), channel_id=1, source_target_pairs={{0,4},{4,8},{8,12},{6,2},{10,6},{14,10},{1,5},{5,9},{9,13},{7,3},{... | collective-permute-start | bytes 1179656 | tf_op jit(solution)/shard_map/ppermute | solution.py:259
  198.9 0.9 copy-done.9
  199.8 10.3 %attend.9 = (bf16[384,256]{1,0:T(8,128)(2,1)S(1)}, bf16[384,256]{1,0:T(8,128)(2,1)S(1)}) custom-call(bf16[768,1536]{1,0:T(8,128)(2,1)} %reorder.1.q_ref, bf16[768,512]{1,0:T(8,128)(2,1)S(1)} %copy-done.1, bf16[768,512]{1,0:T(8,128)(2,1)} %collective-permute-done.refs_1_.refs_4_, bf16[768,512]{1,0:T(8,128)(2,1)} %collective-permute-done.6.refs_2_.refs_5_, ...), custom_call_target="tpu_custom_call" | custom-call | flops 3623878656 | bytes 3145728 | tf_op jit(solution)/shard_map/attend/pallas_call | solution.py:148
  210.2 10.3 %attend.10 = (bf16[384,256]{1,0:T(8,128)(2,1)S(1)}, bf16[384,256]{1,0:T(8,128)(2,1)S(1)}) custom-call(bf16[768,1536]{1,0:T(8,128)(2,1)} %reorder.1.q_ref, bf16[768,512]{1,0:T(8,128)(2,1)S(1)} %copy-done.2, bf16[768,512]{1,0:T(8,128)(2,1)} %collective-permute-done.5.refs_1_.refs_4_, bf16[768,512]{1,0:T(8,128)(2,1)} %collective-permute-done.8.refs_2_.refs_5_, ...), custom_call_target="tpu_custom_call" | custom-call | flops 3623878656 | bytes 3145728 | tf_op jit(solution)/shard_map/attend/pallas_call | solution.py:148
  221.0 10.3 %attend.11 = (bf16[384,256]{1,0:T(8,128)(2,1)S(1)}, bf16[384,256]{1,0:T(8,128)(2,1)S(1)}) custom-call(bf16[768,1536]{1,0:T(8,128)(2,1)} %reorder.1.q_ref, bf16[768,512]{1,0:T(8,128)(2,1)S(1)} %copy-done, bf16[768,512]{1,0:T(8,128)(2,1)} %collective-permute-done.7.refs_1_.refs_4_, bf16[768,512]{1,0:T(8,128)(2,1)S(1)} %collective-permute-done.10.refs_2_.refs_5_, ...), custom_call_target="tpu_custom_call" | custom-call | flops 3623878656 | bytes 3145728 | tf_op jit(solution)/shard_map/attend/pallas_call | solution.py:148
  231.5 42.6 %collective-permute-done.22.refs_17_ = bf16[8,384,384]{2,1,0:T(8,128)(2,1)S(1)} collective-permute-done((bf16[8,384,384]{2,1,0:T(8,128)(2,1)}, bf16[8,384,384]{2,1,0:T(8,128)(2,1)S(1)}, u32[]{:S(2)}, u32[]{:S(2)}) %collective-permute-start.22) | collective-permute-done | bytes 2359328 | tf_op jit(solution)/shard_map/ppermute | solution.py:271
  274.7 3.9 %collective-permute-done.19.refs_11_ = bf16[384,256]{1,0:T(8,128)(2,1)S(1)} collective-permute-done((bf16[384,256]{1,0:T(8,128)(2,1)S(1)}, bf16[384,256]{1,0:T(8,128)(2,1)S(1)}, u32[]{:S(2)}, u32[]{:S(2)}) %collective-permute-start.19) | collective-permute-done | bytes 196640 | tf_op jit(solution)/shard_map/ppermute | solution.py:284
  279.0 1.1 collective-permute-done.18.refs_10_
  280.4 1.1 collective-permute-done.17.refs_9_
  281.9 1.1 collective-permute-done.16.refs_8_
  283.3 4.6 %attend.12 = (bf16[384,128]{1,0:T(8,128)(2,1)S(1)}, bf16[384,128]{1,0:T(8,128)(2,1)S(1)}) custom-call(bf16[768,1536]{1,0:T(8,128)(2,1)S(1)} %copy-done.15, bf16[768,256]{1,0:T(8,128)(2,1)S(1)} %copy-done.6, bf16[768,256]{1,0:T(8,128)(2,1)S(1)} %collective-permute-done.9.refs_1_.refs_4_, bf16[768,256]{1,0:T(8,128)(2,1)S(1)} %collective-permute-done.12.refs_2_.refs_5_, ...), custom_call_target="tpu_custom_call" | custom-call | flops 1811939328 | bytes 1572864 | tf_op jit(solution)/shard_map/attend/pallas_call | solution.py:148
  288.0 4.6 %attend.13 = (bf16[384,128]{1,0:T(8,128)(2,1)S(1)}, bf16[384,128]{1,0:T(8,128)(2,1)S(1)}) custom-call(bf16[768,1536]{1,0:T(8,128)(2,1)S(1)} %copy-done.15, bf16[768,256]{1,0:T(8,128)(2,1)S(1)} %copy-done.5, bf16[768,256]{1,0:T(8,128)(2,1)S(1)} %collective-permute-done.11.refs_1_.refs_4_, bf16[768,256]{1,0:T(8,128)(2,1)S(1)} %collective-permute-done.13.refs_2_.refs_5_, ...), custom_call_target="tpu_custom_call" | custom-call | flops 1811939328 | bytes 1572864 | tf_op jit(solution)/shard_map/attend/pallas_call | solution.py:148
  293.2 0.8 collective-permute-done.21.refs_13_
  294.2 15.9 %project.1 = bf16[384,3072]{1,0:T(8,128)(2,1)} custom-call(s32[1]{0:T(128)} %bitcast.shift_ref, bf16[384,256]{1,0:T(8,128)(2,1)S(1)} %copy-done.17, bf16[384,256]{1,0:T(8,128)(2,1)S(1)} %copy-done.19, bf16[384,256]{1,0:T(8,128)(2,1)S(1)} %get-tuple-element.110.refs_2_, bf16[384,256]{1,0:T(8,128)(2,1)S(1)} %get-tuple-element.118.refs_3_, ...), custom_call_target="tpu_custom_call" | custom-call | flops 7247757312 | bytes 18874368 | tf_op jit(solution)/shard_map/project/pallas_call | solution.py:196
  (87 shorter events, 7.7 us)
Async XLA Ops:
  6.5 113.0 %all-gather.5.cloned.1.call-start = ((), (), s32[]{:S(2)}) async-start(), calls=%async_computation | async-start | bytes 2654208 | tf_op jit(solution)/shard_map/all_gather | solution.py:237
  8.5 164.9 %all-gather.7.cloned.1.call-start = ((), (), s32[]{:S(2)}) async-start(), calls=%async_computation.1 | async-start | bytes 2654208 | tf_op jit(solution)/shard_map/all_gather | solution.py:237
  17.7 6.4 %copy-start.3 = (bf16[768,512]{1,0:T(8,128)(2,1)S(1)}, bf16[768,512]{1,0:T(8,128)(2,1)}, u32[]{:S(2)}) copy-start(bf16[768,512]{1,0:T(8,128)(2,1)} %reorder_pair.8.refs_0_.refs_3_) | copy-start | bytes 2359300
  17.7 6.4 %copy-start.4 = (bf16[768,512]{1,0:T(8,128)(2,1)S(1)}, bf16[768,512]{1,0:T(8,128)(2,1)}, u32[]{:S(2)}) copy-start(bf16[768,512]{1,0:T(8,128)(2,1)} %reorder_pair.7.refs_0_.refs_3_) | copy-start | bytes 2359300
  21.1 74.0 %collective-permute-start = (bf16[768,512]{1,0:T(8,128)(2,1)}, bf16[768,512]{1,0:T(8,128)(2,1)}, u32[]{:S(2)}, u32[]{:S(2)}) collective-permute-start(bf16[768,512]{1,0:T(8,128)(2,1)} %reorder_pair.9.refs_0_.refs_3_), channel_id=1, source_target_pairs={{0,2},{2,0},{4,6},{6,4},{8,10},{10,8},{12,14},{14,12},{1,3},{3,1},... | collective-permute-start | bytes 2359304 | tf_op jit(solution)/shard_map/ppermute | solution.py:258
  24.1 48.7 %collective-permute-start.1 = (bf16[768,512]{1,0:T(8,128)(2,1)S(1)}, bf16[768,512]{1,0:T(8,128)(2,1)}, u32[]{:S(2)}, u32[]{:S(2)}) collective-permute-start(bf16[768,512]{1,0:T(8,128)(2,1)S(1)} %copy-done.3), channel_id=1, source_target_pairs={{0,2},{2,0},{4,6},{6,4},{8,10},{10,8},{12,14},{14,12},{1,3},{3,1},... | collective-permute-start | bytes 2359304 | tf_op jit(solution)/shard_map/ppermute | solution.py:258
  24.2 66.4 %collective-permute-start.3 = (bf16[768,512]{1,0:T(8,128)(2,1)S(1)}, bf16[768,512]{1,0:T(8,128)(2,1)}, u32[]{:S(2)}, u32[]{:S(2)}) collective-permute-start(bf16[768,512]{1,0:T(8,128)(2,1)S(1)} %copy-done.4), channel_id=1, source_target_pairs={{0,2},{2,0},{4,6},{6,4},{8,10},{10,8},{12,14},{14,12},{1,3},{3,1},... | collective-permute-start | bytes 2359304 | tf_op jit(solution)/shard_map/ppermute | solution.py:258
  29.3 5.3 %copy-start.20 = (s32[1,6,27]{2,0,1:T(1,128)S(1)}, s32[1,6,27]{2,0,1:T(1,128)}, u32[]{:S(2)}) copy-start(s32[1,6,27]{2,0,1:T(1,128)} %param.9) | copy-start | bytes 1948
  29.3 80.4 %collective-permute-start.5 = (bf16[768,512]{1,0:T(8,128)(2,1)}, bf16[768,512]{1,0:T(8,128)(2,1)}, u32[]{:S(2)}, u32[]{:S(2)}) collective-permute-start(bf16[768,512]{1,0:T(8,128)(2,1)} %reorder_pair.10.refs_0_.refs_3_), channel_id=1, source_target_pairs={{0,2},{2,0},{4,6},{6,4},{8,10},{10,8},{12,14},{14,12},{1,3},{3,1},... | collective-permute-start | bytes 2359304 | tf_op jit(solution)/shard_map/ppermute | solution.py:258
  32.6 136.7 %collective-permute-start.7 = (bf16[768,512]{1,0:T(8,128)(2,1)}, bf16[768,512]{1,0:T(8,128)(2,1)}, u32[]{:S(2)}, u32[]{:S(2)}) collective-permute-start(bf16[768,512]{1,0:T(8,128)(2,1)} %reorder_pair.11.refs_0_.refs_3_), channel_id=1, source_target_pairs={{0,2},{2,0},{4,6},{6,4},{8,10},{10,8},{12,14},{14,12},{1,3},{3,1},... | collective-permute-start | bytes 2359304 | tf_op jit(solution)/shard_map/ppermute | solution.py:258
  72.9 46.7 %collective-permute-start.2 = (bf16[768,512]{1,0:T(8,128)(2,1)}, bf16[768,512]{1,0:T(8,128)(2,1)}, u32[]{:S(2)}, u32[]{:S(2)}) collective-permute-start(bf16[768,512]{1,0:T(8,128)(2,1)} %collective-permute-done.1.refs_1_.refs_4_), channel_id=1, source_target_pairs={{0,4},{4,8},{8,12},{6,2},{10,6},{14,10},{1,5},{5,9},{9,13},{7,3},{... | collective-permute-start | bytes 2359304 | tf_op jit(solution)/shard_map/ppermute | solution.py:259
  90.5 38.6 %collective-permute-start.4 = (bf16[768,512]{1,0:T(8,128)(2,1)}, bf16[768,512]{1,0:T(8,128)(2,1)}, u32[]{:S(2)}, u32[]{:S(2)}) collective-permute-start(bf16[768,512]{1,0:T(8,128)(2,1)} %collective-permute-done.3.refs_1_.refs_4_), channel_id=1, source_target_pairs={{0,4},{4,8},{8,12},{6,2},{10,6},{14,10},{1,5},{5,9},{9,13},{7,3},{... | collective-permute-start | bytes 2359304 | tf_op jit(solution)/shard_map/ppermute | solution.py:259
  95.1 61.7 %collective-permute-start.6 = (bf16[768,512]{1,0:T(8,128)(2,1)}, bf16[768,512]{1,0:T(8,128)(2,1)}, u32[]{:S(2)}, u32[]{:S(2)}) collective-permute-start(bf16[768,512]{1,0:T(8,128)(2,1)} %collective-permute-done.refs_1_.refs_4_), channel_id=1, source_target_pairs={{0,4},{4,8},{8,12},{6,2},{10,6},{14,10},{1,5},{5,9},{9,13},{7,3},{... | collective-permute-start | bytes 2359304 | tf_op jit(solution)/shard_map/ppermute | solution.py:259
  104.5 24.7 %copy-start.7 = (f32[1,6,18,128]{3,1,2,0:T(8,128)}, f32[1,6,18,128]{3,1,2,0:T(8,128)S(1)}, u32[]{:S(2)}) copy-start(f32[1,6,18,128]{3,1,2,0:T(8,128)S(1)} %copy.11) | copy-start | bytes 165892
  109.7 62.2 %collective-permute-start.8 = (bf16[768,512]{1,0:T(8,128)(2,1)}, bf16[768,512]{1,0:T(8,128)(2,1)}, u32[]{:S(2)}, u32[]{:S(2)}) collective-permute-start(bf16[768,512]{1,0:T(8,128)(2,1)} %collective-permute-done.5.refs_1_.refs_4_), channel_id=1, source_target_pairs={{0,4},{4,8},{8,12},{6,2},{10,6},{14,10},{1,5},{5,9},{9,13},{7,3},{... | collective-permute-start | bytes 2359304 | tf_op jit(solution)/shard_map/ppermute | solution.py:259
  140.7 37.6 %copy-start.6 = (bf16[768,256]{1,0:T(8,128)(2,1)S(1)}, bf16[768,256]{1,0:T(8,128)(2,1)}, u32[]{:S(2)}) copy-start(bf16[768,256]{1,0:T(8,128)(2,1)} %reorder_pair.12.refs_0_.refs_3_) | copy-start | bytes 1179652
  140.7 37.7 %copy-start.5 = (bf16[768,256]{1,0:T(8,128)(2,1)S(1)}, bf16[768,256]{1,0:T(8,128)(2,1)}, u32[]{:S(2)}) copy-start(bf16[768,256]{1,0:T(8,128)(2,1)} %reorder_pair.13.refs_0_.refs_3_) | copy-start | bytes 1179652
  140.7 58.1 %copy-start.1 = (bf16[768,512]{1,0:T(8,128)(2,1)S(1)}, bf16[768,512]{1,0:T(8,128)(2,1)}, u32[]{:S(2)}) copy-start(bf16[768,512]{1,0:T(8,128)(2,1)} %reorder_pair.9.refs_0_.refs_3_) | copy-start | bytes 2359300
  156.8 0.9 copy-start.8
  171.9 59.5 %collective-permute-start.14 = (bf16[8,384,384]{2,1,0:T(8,128)(2,1)}, bf16[8,384,384]{2,1,0:T(8,128)(2,1)}, u32[]{:S(2)}, u32[]{:S(2)}) collective-permute-start(bf16[8,384,384]{2,1,0:T(8,128)(2,1)} %bitcast.1.refs_14_), channel_id=1, source_target_pairs={{0,16},{16,0},{1,17},{17,1},{2,18},{18,2},{3,19},{19,3},{4,20},{20... | collective-permute-start | bytes 7077896 | tf_op jit(solution)/shard_map/ppermute | solution.py:271
  173.4 36.8 %copy-start.2 = (bf16[768,512]{1,0:T(8,128)(2,1)S(1)}, bf16[768,512]{1,0:T(8,128)(2,1)}, u32[]{:S(2)}) copy-start(bf16[768,512]{1,0:T(8,128)(2,1)} %reorder_pair.10.refs_0_.refs_3_) | copy-start | bytes 2359300
  173.4 100.8 %collective-permute-start.22 = (bf16[8,384,384]{2,1,0:T(8,128)(2,1)}, bf16[8,384,384]{2,1,0:T(8,128)(2,1)S(1)}, u32[]{:S(2)}, u32[]{:S(2)}) collective-permute-start(bf16[8,384,384]{2,1,0:T(8,128)(2,1)} %bitcast.19), channel_id=1, source_target_pairs={{0,16},{16,0},{1,17},{17,1},{2,18},{18,2},{3,19},{19,3},{4,20},{20... | collective-permute-start | bytes 7077896 | tf_op jit(solution)/shard_map/ppermute | solution.py:271
  173.9 36.2 %collective-permute-start.10 = (bf16[768,512]{1,0:T(8,128)(2,1)}, bf16[768,512]{1,0:T(8,128)(2,1)S(1)}, u32[]{:S(2)}, u32[]{:S(2)}) collective-permute-start(bf16[768,512]{1,0:T(8,128)(2,1)} %collective-permute-done.7.refs_1_.refs_4_), channel_id=1, source_target_pairs={{0,4},{4,8},{8,12},{6,2},{10,6},{14,10},{1,5},{5,9},{9,13},{7,3},{... | collective-permute-start | bytes 2359304 | tf_op jit(solution)/shard_map/ppermute | solution.py:259
  178.4 12.1 %collective-permute-start.9 = (bf16[768,256]{1,0:T(8,128)(2,1)S(1)}, bf16[768,256]{1,0:T(8,128)(2,1)S(1)}, u32[]{:S(2)}, u32[]{:S(2)}) collective-permute-start(bf16[768,256]{1,0:T(8,128)(2,1)S(1)} %copy-done.6), channel_id=1, source_target_pairs={{0,2},{2,0},{4,6},{6,4},{8,10},{10,8},{12,14},{14,12},{1,3},{3,1},... | collective-permute-start | bytes 1179656 | tf_op jit(solution)/shard_map/ppermute | solution.py:258
  178.5 16.9 %collective-permute-start.11 = (bf16[768,256]{1,0:T(8,128)(2,1)S(1)}, bf16[768,256]{1,0:T(8,128)(2,1)S(1)}, u32[]{:S(2)}, u32[]{:S(2)}) collective-permute-start(bf16[768,256]{1,0:T(8,128)(2,1)S(1)} %copy-done.5), channel_id=1, source_target_pairs={{0,2},{2,0},{4,6},{6,4},{8,10},{10,8},{12,14},{14,12},{1,3},{3,1},... | collective-permute-start | bytes 1179656 | tf_op jit(solution)/shard_map/ppermute | solution.py:258
  190.5 30.1 %collective-permute-start.12 = (bf16[768,256]{1,0:T(8,128)(2,1)S(1)}, bf16[768,256]{1,0:T(8,128)(2,1)S(1)}, u32[]{:S(2)}, u32[]{:S(2)}) collective-permute-start(bf16[768,256]{1,0:T(8,128)(2,1)S(1)} %collective-permute-done.9.refs_1_.refs_4_), channel_id=1, source_target_pairs={{0,4},{4,8},{8,12},{6,2},{10,6},{14,10},{1,5},{5,9},{9,13},{7,3},{... | collective-permute-start | bytes 1179656 | tf_op jit(solution)/shard_map/ppermute | solution.py:259
  195.4 36.0 %collective-permute-start.13 = (bf16[768,256]{1,0:T(8,128)(2,1)S(1)}, bf16[768,256]{1,0:T(8,128)(2,1)S(1)}, u32[]{:S(2)}, u32[]{:S(2)}) collective-permute-start(bf16[768,256]{1,0:T(8,128)(2,1)S(1)} %collective-permute-done.11.refs_1_.refs_4_), channel_id=1, source_target_pairs={{0,4},{4,8},{8,12},{6,2},{10,6},{14,10},{1,5},{5,9},{9,13},{7,3},{... | collective-permute-start | bytes 1179656 | tf_op jit(solution)/shard_map/ppermute | solution.py:259
  198.9 0.9 copy-start.9
  199.7 10.4 %copy-start.21 = (bf16[3072,384]{1,0:T(8,128)(2,1)S(1)}, bf16[3072,384]{1,0:T(8,128)(2,1)}, u32[]{:S(2)}) copy-start(bf16[3072,384]{1,0:T(8,128)(2,1)} %all-gather.7.cloned.1.call-done) | copy-start | bytes 7077892
  199.8 10.5 %copy-start.10 = (f32[1,6,18,128]{3,1,2,0:T(8,128)S(1)}, f32[1,6,18,128]{3,1,2,0:T(8,128)}, u32[]{:S(2)}) copy-start(f32[1,6,18,128]{3,1,2,0:T(8,128)} %copy-done.7) | copy-start | bytes 165892
  210.1 11.0 %copy-start = (bf16[768,512]{1,0:T(8,128)(2,1)S(1)}, bf16[768,512]{1,0:T(8,128)(2,1)}, u32[]{:S(2)}) copy-start(bf16[768,512]{1,0:T(8,128)(2,1)} %reorder_pair.11.refs_0_.refs_3_) | copy-start | bytes 2359300
  210.1 82.7 %collective-permute-start.24 = (bf16[8,384,384]{2,1,0:T(8,128)(2,1)S(1)}, bf16[8,384,384]{2,1,0:T(8,128)(2,1)}, u32[]{:S(2)}, u32[]{:S(2)}) collective-permute-start(bf16[8,384,384]{2,1,0:T(8,128)(2,1)S(1)} %bitcast.21), channel_id=1, source_target_pairs={{0,1},{1,0},{2,3},{3,2},{4,5},{5,4},{6,7},{7,6},{8,9},{9,8},{10,11... | collective-permute-start | bytes 7077896 | tf_op jit(solution)/shard_map/ppermute | solution.py:286
  220.5 61.0 %copy-start.14 = (bf16[384,256]{1,0:T(8,128)(2,1)S(1)}, bf16[384,256]{1,0:T(8,128)(2,1)}, u32[]{:S(2)}) copy-start(bf16[384,256]{1,0:T(8,128)(2,1)} %copy-done.13) | copy-start | bytes 589828
  220.5 62.4 %copy-start.12 = (bf16[384,256]{1,0:T(8,128)(2,1)S(1)}, bf16[384,256]{1,0:T(8,128)(2,1)}, u32[]{:S(2)}) copy-start(bf16[384,256]{1,0:T(8,128)(2,1)} %copy-done.11) | copy-start | bytes 589828
  220.6 62.8 %copy-start.15 = (bf16[768,1536]{1,0:T(8,128)(2,1)S(1)}, bf16[768,1536]{1,0:T(8,128)(2,1)}, u32[]{:S(2)}) copy-start(bf16[768,1536]{1,0:T(8,128)(2,1)} %reorder.1.q_ref) | copy-start | bytes 7077892
  220.6 72.7 %collective-permute-start.23 = (bf16[8,384,384]{2,1,0:T(8,128)(2,1)}, bf16[8,384,384]{2,1,0:T(8,128)(2,1)}, u32[]{:S(2)}, u32[]{:S(2)}) collective-permute-start(bf16[8,384,384]{2,1,0:T(8,128)(2,1)} %bitcast.1.refs_14_), channel_id=1, source_target_pairs={{0,1},{1,0},{2,3},{3,2},{4,5},{5,4},{6,7},{7,6},{8,9},{9,8},{10,11... | collective-permute-start | bytes 7077896 | tf_op jit(solution)/shard_map/ppermute | solution.py:286
  231.4 62.8 %collective-permute-start.25 = (bf16[8,384,384]{2,1,0:T(8,128)(2,1)}, bf16[8,384,384]{2,1,0:T(8,128)(2,1)}, u32[]{:S(2)}, u32[]{:S(2)}) collective-permute-start(bf16[8,384,384]{2,1,0:T(8,128)(2,1)} %collective-permute-done.14.refs_16_), channel_id=1, source_target_pairs={{0,1},{1,0},{2,3},{3,2},{4,5},{5,4},{6,7},{7,6},{8,9},{9,8},{10,11... | collective-permute-start | bytes 7077896 | tf_op jit(solution)/shard_map/ppermute | solution.py:286
  274.2 13.8 %copy-start.22 = (bf16[8,384,384]{2,1,0:T(8,128)(2,1)}, bf16[8,384,384]{2,1,0:T(8,128)(2,1)S(1)}, u32[]{:S(2)}) copy-start(bf16[8,384,384]{2,1,0:T(8,128)(2,1)S(1)} %collective-permute-done.22.refs_17_) | copy-start | bytes 7077892
  274.2 20.0 %collective-permute-start.26 = (bf16[8,384,384]{2,1,0:T(8,128)(2,1)S(1)}, bf16[8,384,384]{2,1,0:T(8,128)(2,1)}, u32[]{:S(2)}, u32[]{:S(2)}) collective-permute-start(bf16[8,384,384]{2,1,0:T(8,128)(2,1)S(1)} %collective-permute-done.22.refs_17_), channel_id=1, source_target_pairs={{0,1},{1,0},{2,3},{3,2},{4,5},{5,4},{6,7},{7,6},{8,9},{9,8},{10,11... | collective-permute-start | bytes 7077896 | tf_op jit(solution)/shard_map/ppermute | solution.py:286
  274.2 4.4 %collective-permute-start.19 = (bf16[384,256]{1,0:T(8,128)(2,1)S(1)}, bf16[384,256]{1,0:T(8,128)(2,1)S(1)}, u32[]{:S(2)}, u32[]{:S(2)}) collective-permute-start(bf16[384,256]{1,0:T(8,128)(2,1)S(1)} %get-tuple-element.150), channel_id=1, source_target_pairs={{0,1},{1,0},{2,3},{3,2},{4,5},{5,4},{6,7},{7,6},{8,9},{9,8},{10,11... | collective-permute-start | bytes 589832 | tf_op jit(solution)/shard_map/ppermute | solution.py:284
  278.6 1.4 collective-permute-start.18
  280.0 1.4 collective-permute-start.17
  281.5 1.4 collective-permute-start.16
  282.9 9.7 %collective-permute-start.15 = (bf16[384,256]{1,0:T(8,128)(2,1)S(1)}, bf16[384,256]{1,0:T(8,128)(2,1)S(1)}, u32[]{:S(2)}, u32[]{:S(2)}) collective-permute-start(bf16[384,256]{1,0:T(8,128)(2,1)S(1)} %copy-done.12), channel_id=1, source_target_pairs={{0,1},{1,0},{2,3},{3,2},{4,5},{5,4},{6,7},{7,6},{8,9},{9,8},{10,11... | collective-permute-start | bytes 589832 | tf_op jit(solution)/shard_map/ppermute | solution.py:284
  288.0 6.2 %copy-start.17 = (bf16[384,256]{1,0:T(8,128)(2,1)S(1)}, bf16[384,256]{1,0:T(8,128)(2,1)}, u32[]{:S(2)}) copy-start(bf16[384,256]{1,0:T(8,128)(2,1)} %copy-done.16) | copy-start | bytes 589828
  288.0 6.2 %copy-start.19 = (bf16[384,256]{1,0:T(8,128)(2,1)S(1)}, bf16[384,256]{1,0:T(8,128)(2,1)}, u32[]{:S(2)}) copy-start(bf16[384,256]{1,0:T(8,128)(2,1)} %copy-done.18) | copy-start | bytes 589828
  292.7 1.4 collective-permute-start.21
  292.9 1.3 collective-permute-start.20
  (4 other events, 2.7 us)
Sparse Core Ops, SparseCore 0:
  9.5 67.6 all-gather.4
  79.4 73.1 all-gather.6
